TPU v7x, 32 devices: a whole 2x2x4 slice. The times are simulated.
32 devices in a mesh: ens: 2 (over x), lat: 16 (over z, y, core).
Axes of the slice: x: 2, y: 2, z: 4, core: 2. Of those that a mesh axis runs over, the one named last changes fastest.
Arguments:
- atmos: bfloat16 [11520, 1024], P(('ens', 'lat')), parts along dimension 0, may hold values from -6 to 6
- ocean_state: bfloat16 [76, 128, 1440], P(None, ('ens', 'lat')), parts along dimension 1, may hold values from -6 to 6
- land_mask: int32 [64, 1440], P('lat'), may hold values 0 or 1
- w_qkv: bfloat16 [1024, 3072], replicated, may hold values from -0.1875 to 0.1875
- w_out: bfloat16 [1024, 1024], replicated, may hold values from -0.1875 to 0.1875
- head_scale: float32 [16], replicated, may hold values from 0.5 to 80
- gain_attn: float32 [1024], replicated, may hold values from 0.5 to 1.5
- gain_flux: float32 [1024], replicated, may hold values from 0.1 to 1.9
- w_flux: bfloat16 [1024, 16], replicated, may hold values from -0.1875 to 0.1875
- surf_embed: float32 [4, 1024], replicated, may hold values from -3 to 3
- flux_start: int32 [64], P('lat'), may hold values from 0 to 14, as said below
- flux_weight: float32 [64, 2], P('lat'), may hold values from 0.25 to 1
- surf_start: int32 [16], P('lat'), may hold values from -2 to 59, as said below
- surf_weight: float32 [16, 7], P('lat'), may hold values from 0.1 to 0.5
- conv_first: bfloat16 [9, 128, 92], replicated, may hold values from -0.21875 to 0.21875
- conv_second: bfloat16 [9, 76, 128], replicated, may hold values from -0.1875 to 0.1875
Outputs:
- atmos_next: bfloat16 [11520, 1024], P(('ens', 'lat')), parts along dimension 0
- ocean_next: bfloat16 [76, 128, 1440], P(None, ('ens', 'lat')), parts along dimension 1
There are 2 independent parts, one for each index of `ens`. A program takes and returns all parts, laid end to end along the dimension named above; an argument that names none is the same for every part. Nothing has to cross between parts.
Inputs may be any that keep to these rules, and one draw needn't show every extreme that they name: flux_start[i] is i // 4 - 1 or i // 4, kept within 0 to 14. surf_start[r] is 4 r - 2 or 4 r - 1.
All inputs are finite; a program needn't handle non-finite values. No bound on the sum of `land_mask` on one device may be relied on, other than what follows from the above.
Results may differ from a plain program's by a relative error of at most 0.0065.
The roundings to bfloat16 on the way count: a program that leaves them out, or rounds other values in their place, can miss the bound.
Values may be sent and summed in bfloat16 or wider, within the bound.
A program may use at most 128 MiB of HBM per device.

v0:
```python
import jax
import jax.numpy as jnp
from jax import lax
from jax.experimental import pallas as pl
from jax.experimental.pallas import tpu as pltpu
from jax.sharding import PartitionSpec as P

LEVELS = 19
VARS = 4
SPAN = 4
OSTEPS = 2


def rms_norm(values, scaling):
    return values * lax.rsqrt(jnp.mean(values * values, axis=-1, keepdims=True) + 1e-06) * scaling


def atmos_kernel(surf_first, surf_weight, flux_first, flux_weight, scale_ref, atmos_ref, top_ref,
                 embed_ref, gain_ref, flux_gain_ref, qkv_ref, wout_ref, wflux_ref, ocean_ref,
                 land_ref,
                 after_ref, flux_mid, flux_low, flux_high, ocean_low, ocean_high, land_low, land_high,
                 surf, near, near_q, near_k, near_v, own_mixed, own_largest, own_total, held, rows,
                 qkv_here, wout_here, load_sems, send_sems, recv_sems):
    me = lax.axis_index("lat")
    count = lax.axis_size("lat")
    token_count, width = atmos_ref.shape
    group = near_q.shape[2]
    groups = width // group
    depth = width // scale_ref.shape[0]
    per_group = group // depth
    has = (me > 0, me < count - 1)
    target = (me - 1, me + 1)

    def send(kind, side, source, dest):
        return pltpu.make_async_remote_copy(
            src_ref=source,
            dst_ref=dest,
            send_sem=send_sems.at[kind, side],
            recv_sem=recv_sems.at[kind, side],
            device_id={"lat": target[side]},
            device_id_type=pl.DeviceIdType.MESH,
        )

    def start_both(kind, source, to_high, to_low):
        @pl.when(has[0])
        def _():
            send(kind, 0, source, to_high).start()

        @pl.when(has[1])
        def _():
            send(kind, 1, source, to_low).start()

    def wait_both(kind, source, to_high, to_low):
        @pl.when(has[0])
        def _():
            send(kind, 1, source, to_low).wait_recv()
            send(kind, 0, source, to_high).wait_send()

        @pl.when(has[1])
        def _():
            send(kind, 0, source, to_high).wait_recv()
            send(kind, 1, source, to_low).wait_send()

    loads = (
        pltpu.make_async_copy(qkv_ref, qkv_here, load_sems.at[0]),
        pltpu.make_async_copy(wout_ref, wout_here, load_sems.at[1]),
    )
    for load in loads:
        load.start()
    barrier = pltpu.get_barrier_semaphore()
    for side in range(2):
        @pl.when(has[side])
        def _(side=side):
            pl.semaphore_signal(
                barrier, inc=1, device_id={"lat": target[side]},
                device_id_type=pl.DeviceIdType.MESH,
            )

    @pl.when(jnp.logical_not(has[0]))
    def _():
        surf[0] = jnp.zeros_like(surf[0])
        near[0] = jnp.zeros_like(near[0])
        rows[0] = jnp.zeros_like(rows[0])
        flux_low[...] = jnp.zeros_like(flux_low)

    @pl.when(jnp.logical_not(has[1]))
    def _():
        surf[2] = jnp.zeros_like(surf[2])
        near[2] = jnp.zeros_like(near[2])
        rows[2] = jnp.zeros_like(rows[2])
        flux_high[...] = jnp.zeros_like(flux_high)

    olon = top_ref.shape[1]
    alon = olon // SPAN
    spans = lax.broadcasted_iota(jnp.int32, (olon, alon), 0) // SPAN
    chosen = spans == lax.broadcasted_iota(jnp.int32, (olon, alon), 1)
    mean = jnp.where(chosen, 1.0, 0.0).astype(jnp.bfloat16)
    surf[1] = (
        jnp.dot(top_ref[...], mean, preferred_element_type=jnp.float32) * (1.0 / SPAN)
    ).astype(jnp.bfloat16)
    pl.semaphore_wait(barrier, jnp.where(has[0], 1, 0) + jnp.where(has[1], 1, 0))
    surf_args = (0, surf.at[1], surf.at[2], surf.at[0])
    start_both(*surf_args)
    wait_both(*surf_args)
    band = jnp.zeros((VARS, surf.shape[2]), jnp.float32)
    for part in range(3):
        block = surf[part].astype(jnp.float32)
        for i in range(block.shape[0] // VARS):
            rows_here = block.shape[0] // VARS
            column = (me + part - 1) * rows_here + i
            weight = jnp.float32(0.0)
            for b in range(surf_weight.shape[1]):
                weight = weight + jnp.where(surf_first[0] + b == column, surf_weight[0, b], 0.0)
            weight = jnp.where((column >= 0) & (column < count * rows_here), weight, 0.0)
            band = band + weight * block[i * VARS : (i + 1) * VARS]
    band = jnp.concatenate([band, jnp.zeros_like(band)], axis=0)
    embed = jnp.concatenate([embed_ref[...], jnp.zeros_like(embed_ref[...])], axis=0)
    started = atmos_ref[...].astype(jnp.float32) + lax.dot_general(
        band, embed, (((0,), (0,)), ((), ())), precision=lax.Precision.HIGHEST,
        preferred_element_type=jnp.float32,
    )
    held[...] = started
    near[1] = rms_norm(started, gain_ref[...]).astype(jnp.bfloat16)
    near_args = (1, near.at[1], near.at[2], near.at[0])
    ocean_args = (2, ocean_ref, ocean_high, ocean_low)
    land_args = (5, land_ref, land_high, land_low)
    start_both(*near_args)

    lane = lax.broadcasted_iota(jnp.int32, (1, group), 1) // depth

    def head_scales(raw):
        squares = raw * raw
        factor = jnp.zeros_like(raw)
        for h in range(per_group):
            total = jnp.sum(jnp.where(lane == h, squares, 0.0), axis=1, keepdims=True)
            factor = jnp.where(lane == h, lax.rsqrt(total * (1.0 / depth) + 1e-06), factor)
        return raw * factor

    def project(part, column):
        return jnp.dot(
            near[part], qkv_here[:, pl.ds(pl.multiple_of(column, group), group)],
            preferred_element_type=jnp.float32,
        )

    def head_scores(queries, h, keys):
        query = jnp.where(lane == h, queries, jnp.zeros_like(queries))
        return lax.dot_general(
            query, keys, (((1,), (1,)), ((), ())), preferred_element_type=jnp.float32
        )

    def own(g, carry):
        column = g * group
        query = head_scales(project(1, column))
        scale = jnp.zeros((1, group), jnp.float32)
        for h in range(per_group):
            scale = jnp.where(lane == h, scale_ref[g * per_group + h], scale)
        near_q[g] = (query * (scale * (1.0 / depth**0.5))).astype(jnp.bfloat16)
        near_k[g, 1] = head_scales(project(1, width + column)).astype(jnp.bfloat16)
        near_v[g, 1] = project(1, 2 * width + column).astype(jnp.bfloat16)
        queries = near_q[g]
        mixed = jnp.zeros((token_count, group), jnp.float32)
        for h in range(per_group):
            score = head_scores(queries, h, near_k[g, 1])
            largest = jnp.max(score, axis=1, keepdims=True)
            raised = jnp.exp(score - largest)
            own_largest[g * per_group + h] = largest
            own_total[g * per_group + h] = jnp.sum(raised, axis=1, keepdims=True)
            value = jnp.dot(
                raised.astype(jnp.bfloat16), near_v[g, 1], preferred_element_type=jnp.float32
            )
            mixed = jnp.where(lane == h, value, mixed)
        own_mixed[g] = mixed
        return carry

    loads[0].wait()
    lax.fori_loop(0, groups, own, 0)
    loads[1].wait()
    wait_both(*near_args)
    start_both(*ocean_args)
    start_both(*land_args)

    def attend(g, carry):
        column = g * group
        for part in (0, 2):
            near_k[g, part] = head_scales(project(part, width + column)).astype(jnp.bfloat16)
            near_v[g, part] = project(part, 2 * width + column).astype(jnp.bfloat16)
        queries = near_q[g]
        mixed = jnp.zeros((token_count, group), jnp.float32)
        for h in range(per_group):
            low = jnp.where(has[0], head_scores(queries, h, near_k[g, 0]), -1e30)
            high = jnp.where(has[1], head_scores(queries, h, near_k[g, 2]), -1e30)
            before = own_largest[g * per_group + h]
            largest = jnp.maximum(
                jnp.max(jnp.maximum(low, high), axis=1, keepdims=True), before
            )
            low = jnp.exp(low - largest)
            high = jnp.exp(high - largest)
            fade = jnp.exp(before - largest)
            total = own_total[g * per_group + h] * fade + jnp.sum(low + high, axis=1, keepdims=True)
            value = jnp.dot(
                low.astype(jnp.bfloat16), near_v[g, 0], preferred_element_type=jnp.float32
            ) + jnp.dot(
                high.astype(jnp.bfloat16), near_v[g, 2], preferred_element_type=jnp.float32
            )
            value = (own_mixed[g] * fade + value) * (1.0 / total)
            mixed = jnp.where(lane == h, value, mixed)
        held[...] += jnp.dot(
            mixed.astype(jnp.bfloat16), wout_here[pl.ds(pl.multiple_of(column, group), group), :],
            preferred_element_type=jnp.float32,
        )
        return carry

    lax.fori_loop(0, groups, attend, 0)
    after = held[...]
    after_ref[...] = after.astype(jnp.bfloat16)
    flux_in = rms_norm(after, flux_gain_ref[...]).astype(jnp.bfloat16)
    rows[1] = lax.dot_general(
        wflux_ref[...], flux_in, (((1,), (1,)), ((), ())), preferred_element_type=jnp.float32
    ).astype(jnp.bfloat16)
    rows_args = (3, rows.at[1], rows.at[2], rows.at[0])
    start_both(*rows_args)
    wait_both(*rows_args)
    sources = [rows[part].astype(jnp.float32) for part in range(3)]
    for i in range(flux_mid.shape[0]):
        regridded = jnp.zeros_like(sources[0])
        for part in range(3):
            weight = jnp.float32(0.0)
            for b in range(flux_weight.shape[1]):
                weight = weight + jnp.where(flux_first[i] + b == me + part - 1, flux_weight[i, b], 0.0)
            regridded = regridded + weight * sources[part]
        flux_mid[i] = regridded.astype(jnp.bfloat16)
    flux_args = (4, flux_mid, flux_high, flux_low)
    start_both(*flux_args)
    wait_both(*ocean_args)
    wait_both(*land_args)
    wait_both(*flux_args)


def atmos_block(surf_start, surf_weight, flux_start, flux_weight, head_scale, atmos, top, gain_attn,
                gain_flux, w_qkv, w_out, w_flux, surf_embed, ocean, land_mask):
    token_count, width = atmos.shape
    alon = top.shape[1] // SPAN
    orows = ocean.shape[0]
    nflux = w_flux.shape[1]
    group = 256
    groups = width // group
    vmem = pl.BlockSpec(memory_space=pltpu.VMEM)
    smem = pl.BlockSpec(memory_space=pltpu.SMEM)
    anywhere = pl.BlockSpec(memory_space=pl.ANY)
    flux_shape = jax.ShapeDtypeStruct((orows, nflux, alon), jnp.bfloat16)
    ocean_shape = jax.ShapeDtypeStruct(ocean.shape, ocean.dtype)
    land_shape = jax.ShapeDtypeStruct(land_mask.shape, land_mask.dtype)
    return pl.pallas_call(
        atmos_kernel,
        out_shape=[
            jax.ShapeDtypeStruct((token_count, width), jnp.bfloat16),
            flux_shape, flux_shape, flux_shape, ocean_shape, ocean_shape, land_shape, land_shape,
        ],
        in_specs=[smem] * 5 + [vmem] * 5 + [anywhere] * 2 + [vmem] + [anywhere] * 2,
        out_specs=[vmem] * 4 + [anywhere] * 4,
        scratch_shapes=[
            pltpu.VMEM((3, top.shape[0], alon), jnp.bfloat16),
            pltpu.VMEM((3, token_count, width), jnp.bfloat16),
            pltpu.VMEM((groups, token_count, group), jnp.bfloat16),
            pltpu.VMEM((groups, 3, token_count, group), jnp.bfloat16),
            pltpu.VMEM((groups, 3, token_count, group), jnp.bfloat16),
            pltpu.VMEM((groups, token_count, group), jnp.float32),
            pltpu.VMEM((head_scale.shape[0], token_count, 1), jnp.float32),
            pltpu.VMEM((head_scale.shape[0], token_count, 1), jnp.float32),
            pltpu.VMEM((token_count, width), jnp.float32),
            pltpu.VMEM((3, nflux, alon), jnp.bfloat16),
            pltpu.VMEM(w_qkv.shape, w_qkv.dtype),
            pltpu.VMEM(w_out.shape, w_out.dtype),
            pltpu.SemaphoreType.DMA((2,)),
            pltpu.SemaphoreType.DMA((6, 2)),
            pltpu.SemaphoreType.DMA((6, 2)),
        ],
        compiler_params=pltpu.CompilerParams(
            collective_id=0, has_side_effects=True, vmem_limit_bytes=58 * 1024 * 1024
        ),
        name="atmos_block",
    )(surf_start, surf_weight, flux_start, flux_weight, head_scale, atmos, top, surf_embed,
      gain_attn[None, :], gain_flux[None, :], w_qkv, w_out, w_flux.T, ocean, land_mask)


def ocean_kernel(low_ref, mid_ref, high_ref, land_low, land_mid, land_high,
                 flux_low, flux_mid, flux_high,
                 first_ref, second_ref, out_ref, xs, hs, st, sea):
    och = mid_ref.shape[1]
    olon = mid_ref.shape[2]
    orows = mid_ref.shape[0]
    wide = xs.shape[1]
    nflux = flux_mid.shape[1]
    hid = first_ref.shape[0] // 3
    opad = second_ref.shape[0] // 3
    stride = opad + nflux
    first_row = lax.axis_index("lat") * orows
    total = lax.axis_size("lat") * orows
    alon = flux_mid.shape[2]
    column = lax.broadcasted_iota(jnp.int32, (alon, wide), 1)
    longitude = jnp.where(column < olon, column, jnp.where(column == olon, 0, olon - 1))
    chosen = longitude // SPAN == lax.broadcasted_iota(jnp.int32, (alon, wide), 0)
    repeat = jnp.where(chosen, 1.0, 0.0).astype(jnp.bfloat16)
    tail = wide - 128
    first_pad = olon - tail

    def wrap(head, last):
        lane = lax.broadcasted_iota(jnp.int32, last.shape, 1)
        end = pltpu.roll(last, 128 - first_pad, 1)
        begin = pltpu.roll(head, first_pad, 1)
        return jnp.where(lane == first_pad, begin, jnp.where(lane == 127, end, last))

    def combine(full, size):
        left = pltpu.roll(full[0:size], 1, 1)
        right = pltpu.roll(full[2 * size : 3 * size], wide - 1, 1)
        return left + full[size : 2 * size] + right

    sides = (
        (low_ref, land_low, flux_low), (mid_ref, land_mid, flux_mid), (high_ref, land_high, flux_high)
    )
    for part, (ref, land, flux) in enumerate(sides):
        def fill(i, carry, ref=ref, land=land, flux=flux, part=part):
            row = part * orows + i
            place = first_row + row - orows
            inside = (place >= 0) & (place < total)
            state = jnp.where(inside, ref[i].astype(jnp.float32), 0.0)
            cells = jnp.where(inside, land[pl.ds(i, 1), :].astype(jnp.float32), 0.0)
            sea[row, :, 0:tail] = cells[:, 0:tail]
            sea[row, :, tail:] = jnp.concatenate(
                [cells[:, tail:], jnp.zeros((1, wide - olon), jnp.float32)], axis=1
            )
            state = jnp.concatenate([state, jnp.zeros((opad - och, olon), jnp.float32)], axis=0)
            last = jnp.concatenate(
                [state[:, tail:], jnp.zeros((opad, wide - olon), jnp.float32)], axis=1
            )
            st[row, :, 0:tail] = state[:, 0:tail]
            st[row, :, tail:] = wrap(state[:, 0:128], last)
            base = pl.multiple_of(row * stride, 16)
            xs[pl.ds(base, opad), :] = st[row].astype(jnp.bfloat16)
            spread = jnp.dot(flux[i], repeat, preferred_element_type=jnp.float32)
            base = pl.multiple_of(row * stride + opad, 16)
            xs[pl.ds(base, nflux), :] = spread.astype(jnp.bfloat16)
            return carry
        lax.fori_loop(0, orows, fill, 0)

    for step in range(OSTEPS):
        edge = 1 + 2 * step

        def first(row, carry):
            block = xs[pl.ds(pl.multiple_of((row - 1) * stride, 16), 3 * stride), :]
            full = jnp.dot(first_ref[...], block, preferred_element_type=jnp.float32)
            hidden = jax.nn.gelu(combine(full, hid), approximate=True)
            place = first_row + row - orows
            inside = jnp.where((place >= 0) & (place < total), 1.0, 0.0).astype(jnp.float32)
            hidden = hidden * inside
            base = pl.multiple_of(row * hid, 16)
            hs[pl.ds(base, hid), 0:tail] = hidden[:, 0:tail].astype(jnp.bfloat16)
            hs[pl.ds(base, hid), tail:] = wrap(hidden[:, 0:128], hidden[:, tail:]).astype(jnp.bfloat16)
            return carry
        lax.fori_loop(edge, 3 * orows - edge, first, 0, unroll=2)

        def second(row, carry):
            block = hs[pl.ds(pl.multiple_of((row - 1) * hid, 16), 3 * hid), :]
            full = jnp.dot(second_ref[...], block, preferred_element_type=jnp.float32)
            state = st[row] + sea[row] * combine(full, opad)
            if step == OSTEPS - 1:
                out_ref[row - orows] = state[0:och, 0:olon].astype(jnp.bfloat16)
            else:
                st[row, :, 0:tail] = state[:, 0:tail]
                st[row, :, tail:] = wrap(state[:, 0:128], state[:, tail:])
                base = pl.multiple_of(row * stride, 16)
                xs[pl.ds(base, opad), :] = st[row].astype(jnp.bfloat16)
            return carry
        lax.fori_loop(edge + 1, 3 * orows - edge - 1, second, 0, unroll=4)


def round_up(value, unit):
    return (value + unit - 1) // unit * unit


def ocean_steps(state_parts, land_parts, fluxes, conv_first, conv_second):
    orows, _, olon = state_parts[1].shape
    och = conv_second.shape[1]
    nflux = fluxes[1].shape[1]
    hid = conv_first.shape[1]
    opad = round_up(och, 16)
    wide = round_up(olon + 2, 128)
    first = conv_first.reshape(3, 3, hid, och + nflux)
    first = jnp.concatenate(
        [first[..., :och], jnp.zeros((3, 3, hid, opad - och), first.dtype), first[..., och:]], axis=3
    )
    first = first.transpose(1, 2, 0, 3).reshape(3 * hid, 3 * (opad + nflux))
    second = jnp.pad(conv_second.reshape(3, 3, och, hid), ((0, 0), (0, 0), (0, opad - och), (0, 0)))
    second = second.transpose(1, 2, 0, 3).reshape(3 * opad, 3 * hid)
    vmem = pl.BlockSpec(memory_space=pltpu.VMEM)
    return pl.pallas_call(
        ocean_kernel,
        out_shape=jax.ShapeDtypeStruct((orows, och, olon), jnp.bfloat16),
        in_specs=[vmem] * 11,
        out_specs=vmem,
        scratch_shapes=[
            pltpu.VMEM((3 * orows * (opad + nflux), wide), jnp.bfloat16),
            pltpu.VMEM((3 * orows * hid, wide), jnp.bfloat16),
            pltpu.VMEM((3 * orows, opad, wide), jnp.float32),
            pltpu.VMEM((3 * orows, 1, wide), jnp.float32),
        ],
        compiler_params=pltpu.CompilerParams(vmem_limit_bytes=60 * 1024 * 1024),
        name="ocean_steps",
    )(*state_parts, *land_parts, *fluxes, first, second)


def local(
    atmos,
    ocean_state,
    land_mask,
    w_qkv,
    w_out,
    head_scale,
    gain_attn,
    gain_flux,
    w_flux,
    surf_embed,
    flux_start,
    flux_weight,
    surf_start,
    surf_weight,
    conv_first,
    conv_second,
):
    orows = ocean_state.shape[1]
    ocean = ocean_state.transpose(1, 0, 2)
    top = ocean_state[::LEVELS].transpose(1, 0, 2).reshape(orows * VARS, -1)
    outs = atmos_block(
        surf_start, surf_weight, flux_start, flux_weight, head_scale, atmos, top, gain_attn,
        gain_flux, w_qkv, w_out, w_flux, surf_embed, ocean, land_mask,
    )
    atmos_next, flux_mid, flux_low, flux_high, ocean_low, ocean_high, land_low, land_high = outs
    ocean_next = ocean_steps(
        [ocean_low, ocean, ocean_high], [land_low, land_mask, land_high],
        [flux_low, flux_mid, flux_high], conv_first, conv_second,
    )
    return (atmos_next, ocean_next.transpose(1, 0, 2))


def solution(mesh):
    in_specs = (
        P(("ens", "lat"), None),
        P(None, ("ens", "lat"), None),
        P("lat", None),
        P(),
        P(),
        P(),
        P(),
        P(),
        P(),
        P(),
        P("lat"),
        P("lat", None),
        P("lat"),
        P("lat", None),
        P(),
        P(),
    )
    out_specs = (P(("ens", "lat"), None), P(None, ("ens", "lat"), None))
    return jax.shard_map(local, mesh=mesh, in_specs=in_specs, out_specs=out_specs, check_vma=False)
```

profile of v0, /device:TPU:20, one launch (start us, length us, event | category | flops | bytes accessed | tf_op | source)
XLA Modules:
  0.0 97.8 jit_solution(7969311225356540643)
XLA Ops:
  0.6 0.0 copy-start.1
  1.3 1.3 %copy.27.flux_weight = f32[4,2]{1,0:T(4,128)} copy(f32[4,2]{0,1:T(2,128)} %param.27) | data formatting | bytes 64 | tf_op args[11]
  2.7 0.8 slice_bitcast_fusion
  3.5 0.6 reshape.19.top_ref
  4.2 2.3 %copy.40 = bf16[76,4,1440]{2,0,1:T(8,128)(2,1)} copy(bf16[76,4,1440]{2,1,0:T(4,128)(2,1)} %param.17) | data formatting | bytes 1751040 | tf_op args[1]
  6.5 0.0 copy-start.2
  6.5 60.3 %atmos_block.1 = (bf16[360,1024]{1,0:T(8,128)(2,1)}, bf16[4,16,360]{2,1,0:T(8,128)(2,1)}, bf16[4,16,360]{2,1,0:T(8,128)(2,1)}, bf16[4,16,360]{2,1,0:T(8,128)(2,1...) custom-call(s32[1]{0:T(128)S(6)} %copy.44.surf_first, ...), custom_call_target="tpu_custom_call" | custom-call | tf_op jit(solution)/shard_map/atmos_block/pallas_call | solution.py:253
  66.7 0.0 copy-start
  66.8 0.0 copy-done.1
  66.8 0.1 copy.33
  67.0 0.1 pad.6.clone
  67.0 0.3 pad_maximum_fusion
  67.4 0.9 copy.31.first_ref
  68.3 0.0 copy-done.2
  68.3 0.1 copy.30
  68.4 0.1 pad.4
  68.5 0.7 copy.42
  69.2 24.9 %ocean_steps.1 = bf16[4,76,1440]{2,1,0:T(8,128)(2,1)} custom-call(bf16[4,76,1440]{2,1,0:T(8,128)(2,1)} %get-tuple-element.11.low_ref, bf16[4,76,1440]{2,1,0:T(8,128)(2,1)} %bitcast.26, bf16[4,76,1440]{2,1,0:T(8,128)(2,1)} %get-tuple-element.12.high_ref, s32[4,1440]{1,0:T(4,128)} %get-tuple-element.13.land_low, s32[4,1440]{1,0:T(4,128)} %land_mid.1, ...), custom_call_target="tpu_custom_call" | custom-call | tf_op jit(solution)/shard_map/ocean_steps/pallas_call | solution.py:396
  94.1 2.9 %copy.32 = bf16[76,4,1440]{2,1,0:T(4,128)(2,1)} copy(bf16[76,4,1440]{2,0,1:T(8,128)(2,1)} %bitcast.27) | data formatting | bytes 1751040
  97.0 0.0 copy-done
  97.0 0.9 copy.45
  (6 shorter events, 0.1 us)
Async XLA Ops:
  0.6 66.1 %copy-start.1 = (bf16[9,128,92]{1,2,0:T(8,128)(2,1)S(1)}, bf16[9,128,92]{1,2,0:T(8,128)(2,1)}, u32[]{:S(2)}) copy-start(bf16[9,128,92]{1,2,0:T(8,128)(2,1)} %param.30) | copy-start | bytes 635908
  6.5 61.9 %copy-start.2 = (bf16[9,76,128]{2,1,0:T(8,128)(2,1)S(1)}, bf16[9,76,128]{2,1,0:T(8,128)(2,1)}, u32[]{:S(2)}) copy-start(bf16[9,76,128]{2,1,0:T(8,128)(2,1)} %param.31) | copy-start | bytes 525316
  66.7 30.2 %copy-start = (bf16[360,1024]{1,0:T(8,128)(2,1)S(1)}, bf16[360,1024]{1,0:T(8,128)(2,1)}, u32[]{:S(2)}) copy-start(bf16[360,1024]{1,0:T(8,128)(2,1)} %get-tuple-element.24) | copy-start | bytes 2211844
where the time goes:
time: 99.6 us; the launch traced here: 97.8 us
  Pallas kernels  85.2 us (86%)
  local copies, waits for them, and re-layouts  10.9 us (11%)
  between operations  1.43 us (1%)
    pallas_call x1, Pallas kernels, atmos_block(): pl.pallas_call(atmos_kernel, out_shape=[jax.ShapeDtypeStruct((token_count...  60.3 us
    pallas_call x1, Pallas kernels, ocean_steps(): pl.pallas_call(ocean_kernel, out_shape=jax.ShapeDtypeStruct((orows, och,...  24.9 us
    unnamed x14, local copies, waits for them, and re-layouts  8.22 us

commit v1 on v0

v1 whole, which is shorter than its diff:
```python
import jax
import jax.numpy as jnp
from jax import lax
from jax.experimental import pallas as pl
from jax.experimental.pallas import tpu as pltpu
from jax.sharding import PartitionSpec as P

LEVELS = 19
VARS = 4
SPAN = 4
OSTEPS = 2
GROUP = 256
CHUNK = 512
FAST, OWN, SLOW = 0, 1, 2


def round_up(value, unit):
    return (value + unit - 1) // unit * unit


def rms_norm(values, scaling):
    return values * lax.rsqrt(jnp.mean(values * values, axis=-1, keepdims=True) + 1e-06) * scaling


def step_kernel(surf_first, surf_weight, flux_first, flux_weight, scale_ref, land_ref, embed_ref,
                gain_ref, flux_gain_ref, wflux_ref, atmos_hbm, ocean_hbm, qkv_hbm, wout_hbm,
                first_hbm, second_hbm,
                after_ref, out_ref,
                ocean_in, atmos_in, first_in, second_in, surf, near, queries, keys, vals, keys_wide,
                vals_wide, probs, largest_at, total_at, rows, mid, land, sea,
                line, xs, fx, hs, st, kept, turned, w_state, w_flux, w_second,
                load_sems, send_sems, recv_sems, kv_send, kv_recv, halo_send, halo_recv):
    me = lax.axis_index("lat")
    count = lax.axis_size("lat")
    odd = me % 2
    even = 1 - odd
    fast = me + 1 - 2 * odd
    slow = me - 1 + 2 * odd
    has_slow = (slow >= 0) & (slow < count)
    target = {FAST: fast, SLOW: slow}
    token_count, width = atmos_in.shape
    groups = width // GROUP
    depth = width // scale_ref.shape[0]
    per_group = GROUP // depth
    key_pad = keys_wide.shape[0] // per_group
    och, orows, olon = ocean_in.shape
    wide = xs.shape[1]
    tiles = wide // 128
    nflux = wflux_ref.shape[0]
    taps, _, hid = first_in.shape
    opad = w_second.shape[0]
    alon = olon // SPAN
    tail = wide - 128
    first_pad = olon - tail
    total_rows = count * orows
    bf16 = jnp.bfloat16
    f32 = jnp.float32

    def send(kind, side, source, dest):
        return pltpu.make_async_remote_copy(
            src_ref=source, dst_ref=dest, send_sem=send_sems.at[kind, side],
            recv_sem=recv_sems.at[kind, side], device_id={"lat": target[side]},
            device_id_type=pl.DeviceIdType.MESH,
        )

    def start_both(kind, source, dest):
        send(kind, FAST, source, dest(FAST)).start()

        @pl.when(has_slow)
        def _():
            send(kind, SLOW, source, dest(SLOW)).start()

    def wait_both(kind, source, dest):
        send(kind, FAST, source, dest(FAST)).wait()

        @pl.when(has_slow)
        def _():
            send(kind, SLOW, source, dest(SLOW)).wait()

    def local_row(place):
        return odd * (place - orows) + even * (2 * orows - 1 - place)

    half_width = qkv_hbm.shape[1] // 2
    loads = (
        pltpu.make_async_copy(ocean_hbm, ocean_in, load_sems.at[0]),
        pltpu.make_async_copy(atmos_hbm, atmos_in, load_sems.at[1]),
        pltpu.make_async_copy(qkv_hbm.at[:, 0:half_width], hs.at[0:width, :], load_sems.at[2]),
        pltpu.make_async_copy(
            qkv_hbm.at[:, half_width:], hs.at[width : 2 * width, :], load_sems.at[3]),
        pltpu.make_async_copy(wout_hbm, hs.at[2 * width : 3 * width, 0:width], load_sems.at[4]),
        pltpu.make_async_copy(first_hbm, first_in, load_sems.at[5]),
        pltpu.make_async_copy(second_hbm, second_in, load_sems.at[6]),
    )
    for load in loads:
        load.start()
    barrier = pltpu.get_barrier_semaphore()
    pl.semaphore_signal(
        barrier, inc=1, device_id={"lat": fast}, device_id_type=pl.DeviceIdType.MESH)

    @pl.when(has_slow)
    def _():
        pl.semaphore_signal(
            barrier, inc=1, device_id={"lat": slow}, device_id_type=pl.DeviceIdType.MESH)

    @pl.when(jnp.logical_not(has_slow))
    def _():
        surf[SLOW] = jnp.zeros_like(surf[SLOW])
        rows[SLOW] = jnp.zeros_like(rows[SLOW])
        mid[SLOW] = jnp.zeros_like(mid[SLOW])
        land[SLOW] = jnp.zeros_like(land[SLOW])
        for i in range(orows):
            base = (2 * orows + i) * 3 * opad + opad
            xs[base : base + opad, :] = jnp.zeros((opad, wide), bf16)

    spans = lax.broadcasted_iota(jnp.int32, (olon, alon), 0) // SPAN
    chosen = spans == lax.broadcasted_iota(jnp.int32, (olon, alon), 1)
    mean = jnp.where(chosen, 1.0, 0.0).astype(bf16)
    loads[0].wait()
    top = jnp.concatenate(
        [ocean_in[v * LEVELS].astype(f32) for v in range(VARS)], axis=0).astype(bf16)
    surf[OWN] = (jnp.dot(top, mean, preferred_element_type=f32) * (1.0 / SPAN)).astype(bf16)
    land[OWN] = land_ref[...]
    pl.semaphore_wait(barrier, 1 + jnp.where(has_slow, 1, 0))

    def surf_at(side):
        return surf.at[side]

    def land_at(side):
        return land.at[side]

    start_both(0, surf.at[OWN], surf_at)
    start_both(1, land_ref, land_at)

    for c in range(opad):
        if c < och:
            cells = jnp.concatenate(
                [ocean_in[c].astype(f32), jnp.zeros((orows, wide - olon), f32)], axis=1)
        else:
            cells = jnp.zeros((orows, wide), f32)
        for t in range(tiles):
            line[pl.ds(t * orows * opad + c, orows, stride=opad), :] = cells[
                :, t * 128 : (t + 1) * 128]
    for place in range(orows, 2 * orows):
        base = place * 3 * opad + opad
        for t in range(tiles):
            at = pl.multiple_of(t * orows * opad + local_row(place) * opad, 16)
            xs[base : base + opad, t * 128 : (t + 1) * 128] = line[pl.ds(at, opad), :].astype(bf16)

    loads[5].wait()
    loads[6].wait()
    turned[...] = jnp.zeros_like(turned)
    row_id = lax.broadcasted_iota(jnp.int32, (opad, hid), 0)
    for k in range(taps):
        source = (odd * (k // 3) + even * (2 - k // 3)) * 3 + k % 3
        tap = first_in[source].astype(f32)
        turned[k * opad : (k + 1) * opad, :] = jnp.where(row_id < och, tap[0:opad], 0.0)
    w_state[...] = turned[...].T.astype(bf16)
    turned[...] = jnp.zeros_like(turned)
    for k in range(taps):
        source = (odd * (k // 3) + even * (2 - k // 3)) * 3 + k % 3
        turned[k * nflux : (k + 1) * nflux, :] = first_in[source].astype(f32)[och:]
        w_second[0:och, k * hid : (k + 1) * hid] = second_in[source]
        w_second[och:, k * hid : (k + 1) * hid] = jnp.zeros((opad - och, hid), bf16)
    w_flux[...] = turned[0 : w_flux.shape[1], :].T.astype(bf16)

    embed = jnp.concatenate(
        [jnp.broadcast_to(embed_ref[v : v + 1, :], (orows, width)) for v in range(VARS)], axis=0)
    which = lax.broadcasted_iota(jnp.int32, (VARS * orows, 1), 0) % orows
    scaled = []
    for device in (fast, me, slow):
        weights = jnp.zeros((VARS * orows, 1), f32)
        for i in range(orows):
            column = device * orows + i
            weight = jnp.float32(0.0)
            for b in range(surf_weight.shape[1]):
                weight = weight + jnp.where(surf_first[0] + b == column, surf_weight[0, b], 0.0)
            weight = jnp.where((column >= 0) & (column < total_rows), weight, 0.0)
            weights = jnp.where(which == i, weight, weights)
        scaled.append(weights * embed)
    scaled = jnp.concatenate(scaled, axis=0)
    high = scaled.astype(bf16)
    rest = scaled - high.astype(f32)
    middle = rest.astype(bf16)
    low = (rest - middle.astype(f32)).astype(bf16)
    scaled = jnp.concatenate([high, middle, low], axis=0)
    loads[1].wait()
    wait_both(0, surf.at[OWN], surf_at)
    fields = jnp.concatenate([surf[FAST], surf[OWN], surf[SLOW]], axis=0)
    fields = jnp.concatenate([fields] * 3, axis=0)
    started = atmos_in[...].astype(f32) + lax.dot_general(
        fields, scaled, (((0,), (0,)), ((), ())), preferred_element_type=f32)
    held = kept.at[0:token_count, 0:width]
    held[...] = started
    near[0] = rms_norm(started, gain_ref[...]).astype(bf16)

    @pl.when(has_slow)
    def _():
        send(2, SLOW, near.at[0], near.at[1]).start()

    lane = lax.broadcasted_iota(jnp.int32, (1, GROUP), 1) // depth
    half_lane = lax.broadcasted_iota(jnp.int32, (1, 128), 1) // depth
    stat_lane = lax.broadcasted_iota(jnp.int32, (1, 128), 1)

    def head_scales(raw):
        pieces = []
        for t in range(GROUP // 128):
            piece = raw[:, t * 128 : (t + 1) * 128]
            squares = piece * piece
            factor = jnp.zeros_like(piece)
            for h in range(128 // depth):
                total = jnp.sum(jnp.where(half_lane == h, squares, 0.0), axis=1, keepdims=True)
                factor = jnp.where(
                    half_lane == h, lax.rsqrt(total * (1.0 / depth) + 1e-06), factor)
            pieces.append(piece * factor)
        return jnp.concatenate(pieces, axis=1)

    def project(part, column):
        at = pl.ds(pl.multiple_of((column // half_width) * width, width), width)
        columns = pl.ds(pl.multiple_of(column % half_width, GROUP), GROUP)
        return jnp.dot(near[part], hs[at, columns], preferred_element_type=f32)

    per_tile = 128 // depth
    gathered = kept.at[token_count : 2 * token_count, 0:width]

    beyond = stat_lane + (key_pad - 128) >= token_count

    def attend(g, key, value, fresh):
        for h in range(per_group):
            columns = slice(h // per_tile * 128, (h // per_tile + 1) * 128)
            at = slice(h * key_pad, h * key_pad + token_count)
            mine = half_lane == h % per_tile
            keys_wide[at, :] = jnp.where(mine, key[:, columns], jnp.zeros((1, 128), bf16))
            vals_wide[at, :] = jnp.where(mine, value[:, columns], jnp.zeros((1, 128), bf16))
        for t in range(per_group // per_tile):
            both = slice(t * per_tile * key_pad, (t + 1) * per_tile * key_pad)
            scores = lax.dot_general(
                queries[g, :, t * 128 : (t + 1) * 128], keys_wide[both, :],
                (((1,), (1,)), ((), ())), preferred_element_type=f32)
            fade = None
            for j in range(per_tile):
                h = t * per_tile + j
                at = g * per_group + h
                base = j * key_pad
                pieces = [scores[:, base + i : base + i + 128] for i in range(0, key_pad, 128)]
                pieces[-1] = jnp.where(beyond, -1e30, pieces[-1])
                largest = pieces[0]
                for piece in pieces[1:]:
                    largest = jnp.maximum(largest, piece)
                largest = jnp.broadcast_to(
                    jnp.max(largest, axis=1, keepdims=True), (token_count, 128))
                if not fresh:
                    before = largest_at[at]
                    largest = jnp.maximum(largest, before)
                raised = [jnp.exp(piece - largest) for piece in pieces]
                total = raised[0]
                for piece in raised[1:]:
                    total = total + piece
                if not fresh:
                    factor = jnp.exp(before - largest)
                    total = total + total_at[at] * factor
                    fade = factor if fade is None else jnp.where(half_lane == j, factor, fade)
                largest_at[at] = largest
                total_at[at] = total
                for i, piece in enumerate(raised):
                    start = h * key_pad + i * 128
                    probs[:, start : start + 128] = piece.astype(bf16)
            mixed = jnp.dot(probs[:, both], vals_wide[both, :], preferred_element_type=f32)
            columns = pl.ds(pl.multiple_of(g * GROUP + t * 128, 128), 128)
            if fresh:
                gathered[:, columns] = mixed
            else:
                gathered[:, columns] = gathered[:, columns] * fade + mixed

    def kv_copy(g, kind):
        ref = (keys, vals)[kind]
        return pltpu.make_async_remote_copy(
            src_ref=ref.at[0, g], dst_ref=ref.at[1, g], send_sem=kv_send.at[kind, g],
            recv_sem=kv_recv.at[kind, g], device_id={"lat": fast},
            device_id_type=pl.DeviceIdType.MESH,
        )

    def halo_copy(side, place):
        goal = {FAST: 2 * orows - 1, SLOW: 4 * orows - 1}[side] - place
        source = xs.at[pl.ds(place * 3 * opad + opad, opad), :]
        dest = xs.at[pl.ds(goal * 3 * opad + opad, opad), :]
        return pltpu.make_async_remote_copy(
            src_ref=source, dst_ref=dest, send_sem=halo_send.at[side, place - orows],
            recv_sem=halo_recv.at[side, place - orows], device_id={"lat": target[side]},
            device_id_type=pl.DeviceIdType.MESH,
        )

    keys_wide[...] = jnp.zeros_like(keys_wide)
    vals_wide[...] = jnp.zeros_like(vals_wide)

    def own(g, carry):
        column = g * GROUP
        query = head_scales(project(0, column))
        scale = jnp.zeros((1, GROUP), f32)
        for h in range(per_group):
            scale = jnp.where(lane == h, scale_ref[g * per_group + h], scale)
        queries[g] = (query * (scale * (1.0 / depth**0.5))).astype(bf16)
        keys[0, g] = head_scales(project(0, width + column)).astype(bf16)
        vals[0, g] = project(0, 2 * width + column).astype(bf16)
        for kind in range(2):
            kv_copy(g, kind).start()
        attend(g, keys[0, g], vals[0, g], True)
        return carry

    loads[2].wait()
    loads[3].wait()
    lax.fori_loop(0, groups, own, 0)
    for place in range(orows, 2 * orows):
        halo_copy(FAST, place).start()

    def from_fast(g, carry):
        for kind in range(2):
            kv_copy(g, kind).wait()
        attend(g, keys[1, g], vals[1, g], False)
        return carry

    lax.fori_loop(0, groups, from_fast, 0)

    @pl.when(has_slow)
    def _():
        send(2, SLOW, near.at[0], near.at[1]).wait()
        for place in (2 * orows - 1, 2 * orows - 2):
            halo_copy(SLOW, place).start()

    def from_slow(g, carry):
        column = g * GROUP
        key = head_scales(project(1, width + column)).astype(bf16)
        value = project(1, 2 * width + column).astype(bf16)
        attend(g, key, value, False)
        return carry

    @pl.when(has_slow)
    def _():
        lax.fori_loop(0, groups, from_slow, 0)

    loads[4].wait()

    def finish(g, carry):
        columns = pl.ds(pl.multiple_of(g * GROUP, GROUP), GROUP)
        factors = []
        for t in range(per_group // per_tile):
            factor = None
            for j in range(per_tile):
                total = jnp.sum(total_at[g * per_group + t * per_tile + j], axis=1, keepdims=True)
                inverse = jnp.broadcast_to(1.0 / total, (token_count, 128))
                factor = inverse if factor is None else jnp.where(half_lane == j, inverse, factor)
            factors.append(factor)
        factor = jnp.concatenate(factors, axis=1)
        mixed = (gathered[:, columns] * factor).astype(bf16)
        at = pl.ds(pl.multiple_of(2 * width + g * GROUP, GROUP), GROUP)
        held[...] += jnp.dot(mixed, hs[at, 0:width], preferred_element_type=f32)
        return carry

    lax.fori_loop(0, groups, finish, 0)
    after = held[...]
    after_ref[...] = after.astype(bf16)
    flux_in = rms_norm(after, flux_gain_ref[...]).astype(bf16)
    rows[OWN] = lax.dot_general(
        wflux_ref[...], flux_in, (((1,), (1,)), ((), ())), preferred_element_type=f32
    ).astype(bf16)

    def rows_at(side):
        return rows.at[side]

    start_both(3, rows.at[OWN], rows_at)

    @pl.when(has_slow)
    def _():
        for place in range(2 * orows - 3, orows - 1, -1):
            halo_copy(SLOW, place).start()

    def spread(ref, base, size):
        center = pl.ds(base + size, size)
        head = ref[center, 0:128]
        last = ref[center, tail:]
        at = lax.broadcasted_iota(jnp.int32, last.shape, 1)
        end = pltpu.roll(last, 128 - first_pad, 1)
        begin = pltpu.roll(head, first_pad, 1)
        last = jnp.where(at == first_pad, begin, jnp.where(at == 127, end, last))
        whole = jnp.concatenate([ref[center, 0:tail], last], axis=1)
        ref[pl.ds(base, size), :] = pltpu.roll(whole, 1, 1)
        ref[pl.ds(base + 2 * size, size), :] = pltpu.roll(whole, wide - 1, 1)

    def spread_state(place, carry):
        spread(xs, pl.multiple_of(place * 3 * opad, 16), opad)
        return carry

    def spread_hidden(place):
        spread(hs, pl.multiple_of((place + 1) * 3 * hid, 16), hid)

    wait_both(1, land_ref, land_at)
    for side, base in ((FAST, 0), (OWN, orows), (SLOW, 2 * orows)):
        for i in range(orows):
            place = base + i
            if side == OWN:
                at = local_row(place)
            else:
                at = odd * i + even * (orows - 1 - i)
            cells = land[side, pl.ds(at, 1), :].astype(f32)
            sea[place, :, 0:tail] = cells[:, 0:tail]
            sea[place, :, tail:] = jnp.concatenate(
                [cells[:, tail:], jnp.zeros((1, wide - olon), f32)], axis=1)
    for place in range(orows, 2 * orows):
        halo_copy(FAST, place).wait()

    @pl.when(has_slow)
    def _():
        for place in (2 * orows - 1, 2 * orows - 2):
            halo_copy(SLOW, place).wait()

    lax.fori_loop(0, 2 * orows + 2, spread_state, 0)

    def state_part(place, n):
        block = xs[pl.ds(pl.multiple_of((place - 1) * 3 * opad, 16), 9 * opad), n : n + CHUNK]
        return jnp.dot(w_state[:, 0 : 9 * opad], block, preferred_element_type=f32)

    def keep_state(place, carry):
        for n in range(0, wide, CHUNK):
            kept[pl.ds(pl.multiple_of((place - 1) * hid, 16), hid), n : n + CHUNK] = state_part(
                place, n)
        return carry

    lax.fori_loop(1, orows + 1, keep_state, 0, unroll=2)
    wait_both(3, rows.at[OWN], rows_at)
    sources = [rows[side].astype(f32) for side in range(3)]
    for i in range(orows):
        at = local_row(orows + i)
        regridded = jnp.zeros_like(sources[0])
        for side, device in ((FAST, fast), (OWN, me), (SLOW, slow)):
            weight = jnp.float32(0.0)
            for b in range(flux_weight.shape[1]):
                weight = weight + jnp.where(
                    flux_first[at] + b == device, flux_weight[at, b], 0.0)
            regridded = regridded + weight * sources[side]
        mid[OWN, i] = regridded.astype(bf16)

    def mid_at(side):
        return mid.at[side]

    start_both(4, mid.at[OWN], mid_at)
    lax.fori_loop(orows + 1, 2 * orows + 1, keep_state, 0, unroll=2)
    wait_both(4, mid.at[OWN], mid_at)
    column = lax.broadcasted_iota(jnp.int32, (alon, wide), 1)
    longitude = jnp.where(column < olon, column, jnp.where(column == olon, 0, olon - 1))
    chosen = longitude // SPAN == lax.broadcasted_iota(jnp.int32, (alon, wide), 0)
    repeat = jnp.where(chosen, 1.0, 0.0).astype(bf16)
    every = [mid[FAST, orows - 1 - i] for i in range(orows)]
    every += [mid[OWN, i] for i in range(orows)]
    every += [mid[SLOW, orows - 1 - i] for i in range(orows)]
    repeated = jnp.dot(
        jnp.concatenate(every, axis=0), repeat, preferred_element_type=f32).astype(bf16)
    for place in range(3 * orows):
        base = place * 3 * nflux
        whole = repeated[place * nflux : (place + 1) * nflux]
        fx[base + nflux : base + 2 * nflux, :] = whole
        fx[base : base + nflux, :] = pltpu.roll(whole, 1, 1)
        fx[base + 2 * nflux : base + 3 * nflux, :] = pltpu.roll(whole, wide - 1, 1)

    @pl.when(has_slow)
    def _():
        for place in range(2 * orows - 3, orows - 1, -1):
            halo_copy(SLOW, place).wait()

    lax.fori_loop(2 * orows + 2, 3 * orows, spread_state, 0)
    root = (2.0 / jnp.pi) ** 0.5

    def inside_of(place):
        row = me * orows + local_row(place)
        return (row >= 0) & (row < total_rows)

    for step in range(OSTEPS):
        edge = 1 + 2 * step

        def first(place, both):
            half = jnp.where(inside_of(place), 0.5, 0.0).astype(f32)
            at = pl.ds(pl.multiple_of((place - 1) * hid, 16), hid)
            for n in range(0, wide, CHUNK):
                if step == 0:
                    block = fx[
                        pl.ds(pl.multiple_of((place - 1) * 3 * nflux, 16), 9 * nflux), n : n + CHUNK]
                    share = jnp.dot(w_flux[...], block, preferred_element_type=f32)
                    full = share + (state_part(place, n) if both else kept[at, n : n + CHUNK])
                    kept[at, n : n + CHUNK] = share
                else:
                    full = kept[at, n : n + CHUNK] + state_part(place, n)
                bent = jnp.tanh(full * (root + (root * 0.044715) * (full * full)))
                half_full = full * half
                hidden = half_full + half_full * bent
                hs[pl.ds(pl.multiple_of((place + 1) * 3 * hid + hid, 16), hid), n : n + CHUNK] = (
                    hidden.astype(bf16))

        def firsts(pair, carry, both=False):
            place = edge + 2 * pair
            for i in (-2, -1):
                spread_hidden(place + i)
            for i in (0, 1):
                first(place + i, both)
            return carry

        pairs = (3 * orows - 2 * edge) // 2
        if step == 0:
            lax.fori_loop(0, pairs - 1, firsts, 0)
            firsts(pairs - 1, 0, True)
        else:
            lax.fori_loop(0, pairs, firsts, 0)
        for i in (-2, -1):
            spread_hidden(3 * orows - edge + i)

        def second(place):
            for n in range(0, wide, CHUNK):
                block = hs[pl.ds(pl.multiple_of(place * 3 * hid, 16), 9 * hid), n : n + CHUNK]
                full = jnp.dot(w_second[...], block, preferred_element_type=f32)
                center = pl.ds(pl.multiple_of(place * 3 * opad + opad, 16), opad)
                if step == 0:
                    before = xs[center, n : n + CHUNK].astype(f32)
                else:
                    before = st[place - 2, :, n : n + CHUNK]
                state = before + sea[place, :, n : n + CHUNK] * full
                if step == OSTEPS - 1:
                    for t in range(CHUNK // 128):
                        at = (n // 128 + t) * orows * opad + local_row(place) * opad
                        line[pl.ds(pl.multiple_of(at, 16), opad), :] = state[
                            :, t * 128 : (t + 1) * 128]
                else:
                    st[place - 2, :, n : n + CHUNK] = state
                    xs[center, n : n + CHUNK] = state.astype(bf16)

        def seconds(pair, carry):
            place = edge + 1 + 2 * pair
            if step < OSTEPS - 1:
                for i in (-2, -1):
                    spread_state(place + i, 0)
            for i in (0, 1):
                second(place + i)
            return carry

        lax.fori_loop(0, (3 * orows - 2 * edge - 2) // 2, seconds, 0)
        if step < OSTEPS - 1:
            for i in (-2, -1):
                spread_state(3 * orows - edge - 1 + i, 0)

    for c in range(och):
        cells = jnp.concatenate(
            [line[pl.ds(t * orows * opad + c, orows, stride=opad), :] for t in range(tiles)], axis=1)
        out_ref[c] = cells[:, 0:olon].astype(bf16)


def local(
    atmos,
    ocean_state,
    land_mask,
    w_qkv,
    w_out,
    head_scale,
    gain_attn,
    gain_flux,
    w_flux,
    surf_embed,
    flux_start,
    flux_weight,
    surf_start,
    surf_weight,
    conv_first,
    conv_second,
):
    token_count, width = atmos.shape
    och, orows, olon = ocean_state.shape
    alon = olon // SPAN
    nflux = w_flux.shape[1]
    taps, hid, _ = conv_first.shape
    groups = width // GROUP
    per_group = GROUP // (width // head_scale.shape[0])
    key_pad = round_up(token_count, 128)
    opad = round_up(och, 16)
    wide = round_up(olon + 2, CHUNK)
    places = 3 * orows
    bf16 = jnp.bfloat16
    f32 = jnp.float32
    vmem = pl.BlockSpec(memory_space=pltpu.VMEM)
    smem = pl.BlockSpec(memory_space=pltpu.SMEM)
    anywhere = pl.BlockSpec(memory_space=pl.ANY)
    turned_shape = (round_up(taps * opad, 128), hid)
    return pl.pallas_call(
        step_kernel,
        out_shape=[
            jax.ShapeDtypeStruct(atmos.shape, bf16),
            jax.ShapeDtypeStruct(ocean_state.shape, bf16),
        ],
        in_specs=[smem] * 5 + [vmem] * 5 + [anywhere] * 6,
        out_specs=[vmem] * 2,
        scratch_shapes=[
            pltpu.VMEM(ocean_state.shape, bf16),
            pltpu.VMEM(atmos.shape, bf16),
            pltpu.VMEM((taps, och + nflux, hid), bf16),
            pltpu.VMEM(conv_second.shape, bf16),
            pltpu.VMEM((3, VARS * orows, alon), bf16),
            pltpu.VMEM((2, token_count, width), bf16),
            pltpu.VMEM((groups, token_count, GROUP), bf16),
            pltpu.VMEM((2, groups, token_count, GROUP), bf16),
            pltpu.VMEM((2, groups, token_count, GROUP), bf16),
            pltpu.VMEM((per_group * key_pad, 128), bf16),
            pltpu.VMEM((per_group * key_pad, 128), bf16),
            pltpu.VMEM((token_count, per_group * key_pad), bf16),
            pltpu.VMEM((head_scale.shape[0], token_count, 128), f32),
            pltpu.VMEM((head_scale.shape[0], token_count, 128), f32),
            pltpu.VMEM((3, nflux, alon), bf16),
            pltpu.VMEM((3, orows, nflux, alon), bf16),
            pltpu.VMEM((3, orows, olon), jnp.int32),
            pltpu.VMEM((places, 1, wide), f32),
            pltpu.VMEM((wide // 128 * orows * opad, 128), f32),
            pltpu.VMEM((places * 3 * opad, wide), bf16),
            pltpu.VMEM((places * 3 * nflux, wide), bf16),
            pltpu.VMEM((places * 3 * hid, wide), bf16),
            pltpu.VMEM((places - 4, opad, wide), f32),
            pltpu.VMEM(((places - 2) * hid, wide), f32),
            pltpu.VMEM(turned_shape, f32),
            pltpu.VMEM((hid, turned_shape[0]), bf16),
            pltpu.VMEM((hid, taps * nflux), bf16),
            pltpu.VMEM((opad, taps * hid), bf16),
            pltpu.SemaphoreType.DMA((7,)),
            pltpu.SemaphoreType.DMA((5, 3)),
            pltpu.SemaphoreType.DMA((5, 3)),
            pltpu.SemaphoreType.DMA((2, groups)),
            pltpu.SemaphoreType.DMA((2, groups)),
            pltpu.SemaphoreType.DMA((3, orows)),
            pltpu.SemaphoreType.DMA((3, orows)),
        ],
        compiler_params=pltpu.CompilerParams(
            collective_id=0, has_side_effects=True, vmem_limit_bytes=63 * 1024 * 1024
        ),
        name="coupled_step",
    )(surf_start, surf_weight, flux_start, flux_weight, head_scale, land_mask, surf_embed,
      gain_attn[None, :], gain_flux[None, :], w_flux.T, atmos, ocean_state, w_qkv, w_out,
      conv_first.transpose(0, 2, 1), conv_second)


def solution(mesh):
    in_specs = (
        P(("ens", "lat"), None),
        P(None, ("ens", "lat"), None),
        P("lat", None),
        P(),
        P(),
        P(),
        P(),
        P(),
        P(),
        P(),
        P("lat"),
        P("lat", None),
        P("lat"),
        P("lat", None),
        P(),
        P(),
    )
    out_specs = (P(("ens", "lat"), None), P(None, ("ens", "lat"), None))
    return jax.shard_map(local, mesh=mesh, in_specs=in_specs, out_specs=out_specs, check_vma=False)
```

time: 99.6 us -> 77.4 us (0.78)
  Pallas kernels: 85.2 us -> 69.4 us
  local copies, waits for them, and re-layouts: 10.9 us -> 5.8 us
    pallas_call x2 -> x1, Pallas kernels: 85.2 us -> 69.4 us  [local(): pl.pallas_call(step_kernel, out_shape=[jax.ShapeDtypeStruct(atmos.shape,...]
    unnamed x14 -> x3, local copies, waits for them, and re-layouts: 8.22 us -> 5.8 us
    reshape x3 -> x0, local copies, waits for them, and re-layouts: 1.63 us -> none  [the longest x1 0.89 us: ocean_steps(): first = first.transpose(1, 2, 0, 3).reshape(3 * hid, 3 * (opad + nflux))]
where the time goes in v1:
time: 77.4 us; the launch traced here: 76.5 us
  Pallas kernels  69.4 us (90%)
  local copies, waits for them, and re-layouts  5.8 us (7%)
  between operations  1.29 us (2%)
    pallas_call x1, Pallas kernels, local(): pl.pallas_call(step_kernel, out_shape=[jax.ShapeDtypeStruct(atmos.shape,...  69.4 us
    unnamed x3, local copies, waits for them, and re-layouts  5.8 us

profile of v1, /device:TPU:20, one launch (start us, length us, event | category | flops | bytes accessed | tf_op | source)
XLA Modules:
  0.0 76.5 jit_solution(10242064348976842306)
XLA Ops:
  1.3 1.3 %copy.18.flux_weight = f32[4,2]{1,0:T(4,128)} copy(f32[4,2]{0,1:T(2,128)} %param.27) | data formatting | bytes 64 | tf_op args[11]
  2.6 69.4 %coupled_step.1 = (bf16[360,1024]{1,0:T(8,128)(2,1)}, bf16[76,4,1440]{2,1,0:T(4,128)(2,1)}) custom-call(s32[1]{0:T(128)S(6)} %copy.21.surf_first, f32[1,7]{1,0:T(1,128)} %surf_weight.1, s32[4]{0:T(128)} %flux_first.1, f32[4,2]{1,0:T(4,128)} %copy.18.flux_weight, f32[16]{0:T(128)} %scale_ref.1, s32[4,1440]{1,0:T(4,128)} %land_ref.1, f32[4,1024]{1,0:T(4,128)} %embed_ref.1, ...), custom_call_target="tpu_custom_call" | custom-call | tf_op jit(solution)/shard_map/coupled_step/pallas_call | solution.py:587
  72.1 2.0 %copy.22 = bf16[360,1024]{1,0:T(8,128)(2,1)} copy(bf16[360,1024]{1,0:T(8,128)(2,1)} %get-tuple-element.4) | data formatting | bytes 1474560
  74.1 2.4 %copy.23 = bf16[76,4,1440]{2,1,0:T(4,128)(2,1)} copy(bf16[76,4,1440]{2,1,0:T(4,128)(2,1)} %get-tuple-element.5) | data formatting | bytes 1751040

commit v2 on v1

v2 whole, which is shorter than its diff:
```python
import jax
import jax.numpy as jnp
from jax import lax
from jax.experimental import pallas as pl
from jax.experimental.pallas import tpu as pltpu
from jax.sharding import PartitionSpec as P

LEVELS = 19
VARS = 4
SPAN = 4
OSTEPS = 2
GROUP = 256
CHUNK = 512
FAST, OWN, SLOW = 0, 1, 2


def round_up(value, unit):
    return (value + unit - 1) // unit * unit


def rms_norm(values, scaling):
    return values * lax.rsqrt(jnp.mean(values * values, axis=-1, keepdims=True) + 1e-06) * scaling


def step_kernel(surf_first, surf_weight, flux_first, flux_weight, scale_ref, land_ref, embed_ref,
                gain_ref, flux_gain_ref, wflux_ref, atmos_hbm, ocean_hbm, qkv_hbm, wout_hbm,
                first_hbm, second_hbm,
                after_hbm, line_hbm,
                ocean_in, atmos_in, atmos_near, fields, factors, edge, first_in, second_in, surf, near, queries, keys, vals, keys_wide,
                vals_wide, probs, largest_at, gathered, repeat, rows, mid, land, sea,
                after_out, line, xs, fx, hs, st, kept, turned, w_state, w_flux, w_second,
                load_sems, out_sems, send_sems, recv_sems, kv_send, kv_recv, halo_send, halo_recv):
    me = lax.axis_index("lat")
    count = lax.axis_size("lat")
    odd = me % 2
    even = 1 - odd
    fast = me + 1 - 2 * odd
    slow = me - 1 + 2 * odd
    has_slow = (slow >= 0) & (slow < count)
    target = {FAST: fast, SLOW: slow}
    token_count, width = atmos_in.shape
    groups = width // GROUP
    depth = width // scale_ref.shape[0]
    per_group = GROUP // depth
    padded = near.shape[1]
    per_tile = 128 // depth
    key_pad = keys_wide.shape[1] // per_group
    och, orows, olon = ocean_in.shape
    wide = xs.shape[1]
    tiles = wide // 128
    nflux = wflux_ref.shape[0]
    taps, _, hid = first_in.shape
    opad = w_second.shape[0]
    alon = olon // SPAN
    tail = wide - 128
    first_pad = olon - tail
    total_rows = count * orows
    bf16 = jnp.bfloat16
    f32 = jnp.float32

    def send(kind, side, source, dest):
        return pltpu.make_async_remote_copy(
            src_ref=source, dst_ref=dest, send_sem=send_sems.at[kind, side],
            recv_sem=recv_sems.at[kind, side], device_id={"lat": target[side]},
            device_id_type=pl.DeviceIdType.MESH,
        )

    def start_both(kind, source, dest):
        send(kind, FAST, source, dest(FAST)).start()

        @pl.when(has_slow)
        def _():
            send(kind, SLOW, source, dest(SLOW)).start()

    def wait_both(kind, source, dest):
        send(kind, FAST, source, dest(FAST)).wait()

        @pl.when(has_slow)
        def _():
            send(kind, SLOW, source, dest(SLOW)).wait()

    def local_row(place):
        return odd * (place - orows) + even * (2 * orows - 1 - place)

    half_width = qkv_hbm.shape[1] // 2
    loads = (
        pltpu.make_async_copy(ocean_hbm, ocean_in, load_sems.at[0]),
        pltpu.make_async_copy(atmos_hbm, atmos_in, load_sems.at[1]),
        pltpu.make_async_copy(qkv_hbm.at[:, 0:half_width], hs.at[0:width, :], load_sems.at[2]),
        pltpu.make_async_copy(
            qkv_hbm.at[:, half_width:], hs.at[width : 2 * width, :], load_sems.at[3]),
        pltpu.make_async_copy(wout_hbm, hs.at[2 * width : 3 * width, 0:width], load_sems.at[4]),
        pltpu.make_async_copy(first_hbm, first_in, load_sems.at[5]),
        pltpu.make_async_copy(second_hbm, second_in, load_sems.at[6]),
    )
    for load in loads:
        load.start()
    barrier = pltpu.get_barrier_semaphore()
    pl.semaphore_signal(
        barrier, inc=1, device_id={"lat": fast}, device_id_type=pl.DeviceIdType.MESH)

    @pl.when(has_slow)
    def _():
        pl.semaphore_signal(
            barrier, inc=1, device_id={"lat": slow}, device_id_type=pl.DeviceIdType.MESH)

    @pl.when(jnp.logical_not(has_slow))
    def _():
        surf[SLOW] = jnp.zeros_like(surf[SLOW])
        rows[SLOW] = jnp.zeros_like(rows[SLOW])
        mid[SLOW] = jnp.zeros_like(mid[SLOW])
        land[SLOW] = jnp.zeros_like(land[SLOW])
        for i in range(orows):
            base = (2 * orows + i) * 3 * opad + opad
            xs[base : base + opad, :] = jnp.zeros((opad, wide), bf16)

    column = lax.broadcasted_iota(jnp.int32, (alon, wide), 1)
    longitude = jnp.where(column < olon, column, jnp.where(column == olon, 0, olon - 1))
    first_column = lax.broadcasted_iota(jnp.int32, (alon, wide), 0) * SPAN
    chosen = (longitude >= first_column) & (longitude < first_column + SPAN)
    repeat[...] = jnp.where(chosen, 1.0, 0.0).astype(bf16)
    loads[0].wait()
    top = jnp.concatenate(
        [ocean_in[v * LEVELS].astype(f32) for v in range(VARS)], axis=0).astype(bf16)
    summed = lax.dot_general(
        top, repeat[:, 0:olon], (((1,), (1,)), ((), ())), preferred_element_type=f32)
    surf[OWN] = (summed * (1.0 / SPAN)).astype(bf16)
    land[OWN] = land_ref[...]
    pl.semaphore_wait(barrier, 1 + jnp.where(has_slow, 1, 0))

    def surf_at(side):
        return surf.at[side]

    def land_at(side):
        return land.at[side]

    start_both(0, surf.at[OWN], surf_at)

    @pl.when(has_slow)
    def _():
        send(2, SLOW, atmos_hbm, atmos_near).start()

    start_both(1, land_ref, land_at)

    for c in range(opad):
        if c < och:
            cells = jnp.concatenate(
                [ocean_in[c].astype(f32), jnp.zeros((orows, wide - olon), f32)], axis=1)
        else:
            cells = jnp.zeros((orows, wide), f32)
        for t in range(tiles):
            line[t, pl.ds(c, orows, stride=opad), :] = cells[
                :, t * 128 : (t + 1) * 128]
    for place in range(orows, 2 * orows):
        base = place * 3 * opad + opad
        for t in range(tiles):
            at = pl.multiple_of(local_row(place) * opad, 16)
            xs[base : base + opad, t * 128 : (t + 1) * 128] = line[t, pl.ds(at, opad), :].astype(bf16)
        if place < 2 * orows - 2:
            edge[place - orows] = xs[base : base + opad, :]

    def spread(ref, base, size):
        center = pl.ds(base + size, size)
        head = ref[center, 0:128]
        last = ref[center, tail:]
        at = lax.broadcasted_iota(jnp.int32, last.shape, 1)
        end = pltpu.roll(last, 128 - first_pad, 1)
        begin = pltpu.roll(head, first_pad, 1)
        last = jnp.where(at == first_pad, begin, jnp.where(at == 127, end, last))
        whole = jnp.concatenate([ref[center, 0:tail], last], axis=1)
        ref[pl.ds(base, size), :] = pltpu.roll(whole, 1, 1)
        ref[pl.ds(base + 2 * size, size), :] = pltpu.roll(whole, wide - 1, 1)

    def spread_state(place, carry):
        spread(xs, pl.multiple_of(place * 3 * opad, 16), opad)
        return carry

    def spread_hidden(place):
        spread(hs, pl.multiple_of((place + 1) * 3 * hid, 16), hid)

    lane = lax.broadcasted_iota(jnp.int32, (1, GROUP), 1) // depth
    half_lane = lax.broadcasted_iota(jnp.int32, (1, 128), 1) // depth
    stat_lane = lax.broadcasted_iota(jnp.int32, (1, 128), 1)

    keys_wide[...] = jnp.zeros_like(keys_wide)
    vals_wide[...] = jnp.zeros_like(vals_wide)
    for h in range(per_group):
        counted = jnp.where(half_lane == h % per_tile, 1.0, 0.0).astype(bf16)
        for slot in range(2):
            vals_wide[slot, h * key_pad : h * key_pad + padded, 128:] = jnp.broadcast_to(
                counted, (padded, 128))

    lax.fori_loop(orows, 2 * orows, spread_state, 0)

    loads[5].wait()
    loads[6].wait()
    turned[...] = jnp.zeros_like(turned)
    row_id = lax.broadcasted_iota(jnp.int32, (opad, hid), 0)
    for k in range(taps):
        source = (odd * (k // 3) + even * (2 - k // 3)) * 3 + k % 3
        tap = first_in[source].astype(f32)
        turned[k * opad : (k + 1) * opad, :] = jnp.where(row_id < och, tap[0:opad], 0.0)
    w_state[...] = turned[...].T.astype(bf16)
    turned[...] = jnp.zeros_like(turned)
    for k in range(taps):
        source = (odd * (k // 3) + even * (2 - k // 3)) * 3 + k % 3
        turned[k * nflux : (k + 1) * nflux, :] = first_in[source].astype(f32)[och:]
        w_second[0:och, k * hid : (k + 1) * hid] = second_in[source]
        w_second[och:, k * hid : (k + 1) * hid] = jnp.zeros((opad - och, hid), bf16)
    w_flux[...] = turned[0 : w_flux.shape[1], :].T.astype(bf16)

    embed = jnp.concatenate(
        [jnp.broadcast_to(embed_ref[v : v + 1, :], (orows, width)) for v in range(VARS)], axis=0)
    which = lax.broadcasted_iota(jnp.int32, (VARS * orows, 128), 0) % orows
    for part, device in enumerate((fast, me, slow)):
        weights = jnp.zeros((VARS * orows, 128), f32)
        for i in range(orows):
            column = device * orows + i
            weight = jnp.float32(0.0)
            for b in range(surf_weight.shape[1]):
                weight = weight + jnp.where(surf_first[0] + b == column, surf_weight[0, b], 0.0)
            weight = jnp.where((column >= 0) & (column < total_rows), weight, 0.0)
            weights = jnp.where(which == i, weight, weights)
        factors[0, part * VARS * orows : (part + 1) * VARS * orows, :] = weights

    def start_of(tokens, whose):
        scaled = factors[whose, :, 0:1] * jnp.concatenate([embed] * 3, axis=0)
        high = scaled.astype(bf16)
        rest = scaled - high.astype(f32)
        middle = rest.astype(bf16)
        low = (rest - middle.astype(f32)).astype(bf16)
        started = tokens[...].astype(f32) + lax.dot_general(
            jnp.concatenate([fields[whose]] * 3, axis=0),
            jnp.concatenate([high, middle, low], axis=0),
            (((0,), (0,)), ((), ())), preferred_element_type=f32)
        return jnp.concatenate([started, jnp.zeros((padded - token_count, width), f32)], axis=0)

    loads[1].wait()
    wait_both(0, surf.at[OWN], surf_at)
    fields[0] = jnp.concatenate([surf[FAST], surf[OWN], surf[SLOW]], axis=0)
    started = start_of(atmos_in, 0)
    held = kept.at[0:padded, 0:width]
    held[...] = started
    near[0] = rms_norm(started, gain_ref[...]).astype(bf16)

    def halo_copy(side, place):
        goal = {FAST: 2 * orows - 1, SLOW: 4 * orows - 1}[side] - place
        source = xs.at[pl.ds(place * 3 * opad + opad, opad), :]
        if side == SLOW and place < 2 * orows - 2:
            source = edge.at[place - orows]
        dest = xs.at[pl.ds(goal * 3 * opad + opad, opad), :]
        return pltpu.make_async_remote_copy(
            src_ref=source, dst_ref=dest, send_sem=halo_send.at[side, place - orows],
            recv_sem=halo_recv.at[side, place - orows], device_id={"lat": target[side]},
            device_id_type=pl.DeviceIdType.MESH,
        )

    @pl.when(has_slow)
    def _():
        send(5, SLOW, fields.at[0], fields.at[1]).start()
        send(6, SLOW, factors.at[0], factors.at[1]).start()

    middle_row = round_up(padded // 2, 16)
    blocks = (slice(0, middle_row), slice(middle_row, padded))
    ones_at = lax.broadcasted_iota(jnp.int32, (GROUP, 128), 0) % 128 // depth
    ones = jnp.where(ones_at == half_lane, 1.0, 0.0).astype(bf16)

    def head_scales(raw):
        pieces = []
        for t in range(GROUP // 128):
            piece = raw[:, t * 128 : (t + 1) * 128]
            squares = piece * piece
            coarse = squares.astype(bf16)
            fine = (squares - coarse.astype(f32)).astype(bf16)
            total = jnp.dot(
                jnp.concatenate([coarse, fine], axis=1), ones, preferred_element_type=f32)
            pieces.append(piece * lax.rsqrt(total * (1.0 / depth) + 1e-06))
        return jnp.concatenate(pieces, axis=1)

    def project(part, column, block):
        at = pl.ds(pl.multiple_of((column // half_width) * width, width), width)
        columns = pl.ds(pl.multiple_of(column % half_width, GROUP), GROUP)
        return jnp.dot(near[part, block, :], hs[at, columns], preferred_element_type=f32)

    beyond = stat_lane + (key_pad - 128) >= token_count

    def attend(g, key, value, fresh, slot):
        for h in range(per_group):
            columns = slice(h // per_tile * 128, (h // per_tile + 1) * 128)
            at = slice(h * key_pad, h * key_pad + padded)
            mine = half_lane == h % per_tile
            keys_wide[slot, at, :] = jnp.where(mine, key[:, columns], jnp.zeros((1, 128), bf16))
            vals_wide[slot, at, 0:128] = jnp.where(
                mine, value[:, columns], jnp.zeros((1, 128), bf16))
        for t in range(per_group // per_tile):
            both = slice(t * per_tile * key_pad, (t + 1) * per_tile * key_pad)
            where = g * (per_group // per_tile) + t
            for block in blocks:
                size = block.stop - block.start
                scores = lax.dot_general(
                    queries[g, block, t * 128 : (t + 1) * 128], keys_wide[slot, both, :],
                    (((1,), (1,)), ((), ())), preferred_element_type=f32)
                fade = None
                raised = []
                for j in range(per_tile):
                    at = g * per_group + t * per_tile + j
                    base = j * key_pad
                    pieces = [scores[:, base + i : base + i + 128] for i in range(0, key_pad, 128)]
                    pieces[-1] = jnp.where(beyond, -1e30, pieces[-1])
                    largest = pieces[0]
                    for piece in pieces[1:]:
                        largest = jnp.maximum(largest, piece)
                    largest = jnp.broadcast_to(jnp.max(largest, axis=1, keepdims=True), (size, 128))
                    if not fresh:
                        before = largest_at[at, block, :]
                        largest = jnp.maximum(largest, before)
                        factor = jnp.exp(before - largest)
                        fade = factor if fade is None else jnp.where(half_lane == j, factor, fade)
                    largest_at[at, block, :] = largest
                    raised += [jnp.exp(piece - largest) for piece in pieces]
                probs[slot, block, both] = jnp.concatenate(raised, axis=1).astype(bf16)
                mixed = jnp.dot(
                    probs[slot, block, both], vals_wide[slot, both, :], preferred_element_type=f32)
                if fresh:
                    gathered[where, block, :] = mixed
                else:
                    gathered[where, block, 0:128] = (
                        gathered[where, block, 0:128] * fade + mixed[:, 0:128])
                    gathered[where, block, 128:] = (
                        gathered[where, block, 128:] * fade + mixed[:, 128:])

    def kv_copy(g, kind):
        ref = (keys, vals)[kind]
        return pltpu.make_async_remote_copy(
            src_ref=ref.at[0, g], dst_ref=ref.at[1, g], send_sem=kv_send.at[kind, g],
            recv_sem=kv_recv.at[kind, g], device_id={"lat": fast},
            device_id_type=pl.DeviceIdType.MESH,
        )

    def by_two(body):
        def run(i, carry):
            for slot in range(2):
                body(2 * i + slot, slot)
            return carry
        lax.fori_loop(0, groups // 2, run, 0)

    def own(g, slot):
        column = g * GROUP
        scale = jnp.zeros((1, GROUP), f32)
        for h in range(per_group):
            scale = jnp.where(lane == h, scale_ref[g * per_group + h], scale)
        for block in blocks:
            query = head_scales(project(0, column, block))
            queries[g, block, :] = (query * (scale * (1.0 / depth**0.5))).astype(bf16)
            keys[0, g, block, :] = head_scales(project(0, width + column, block)).astype(bf16)
            vals[0, g, block, :] = project(0, 2 * width + column, block).astype(bf16)
        for kind in range(2):
            kv_copy(g, kind).start()
        attend(g, keys[0, g], vals[0, g], True, slot)

    loads[2].wait()
    loads[3].wait()
    by_two(own)
    for place in range(orows, 2 * orows):
        halo_copy(FAST, place).start()

    def from_fast(g, slot):
        for kind in range(2):
            kv_copy(g, kind).wait()
        attend(g, keys[1, g], vals[1, g], False, slot)

    by_two(from_fast)

    @pl.when(has_slow)
    def _():
        send(2, SLOW, atmos_hbm, atmos_near).wait()
        send(5, SLOW, fields.at[0], fields.at[1]).wait()
        send(6, SLOW, factors.at[0], factors.at[1]).wait()
        for place in (2 * orows - 1, 2 * orows - 2):
            halo_copy(SLOW, place).start()
        near[1] = rms_norm(start_of(atmos_near, 1), gain_ref[...]).astype(bf16)

    def fast_rows(i, carry):
        halo_copy(FAST, orows + i).wait()
        return spread_state(orows - 1 - i, carry)

    def from_slow(g, slot):
        column = g * GROUP
        key = jnp.concatenate(
            [head_scales(project(1, width + column, block)) for block in blocks], axis=0).astype(bf16)
        value = jnp.concatenate(
            [project(1, 2 * width + column, block) for block in blocks], axis=0).astype(bf16)
        attend(g, key, value, False, slot)

    @pl.when(has_slow)
    def _():
        by_two(from_slow)

    lax.fori_loop(0, orows, fast_rows, 0)
    loads[4].wait()

    for t in range(width // 128):
        near[0, :, t * 128 : (t + 1) * 128] = (
            gathered[t, :, 0:128] * (1.0 / gathered[t, :, 128:])).astype(bf16)
    pieces = []
    for n in range(0, width, CHUNK):
        piece = held[:, n : n + CHUNK] + jnp.dot(
            near[0], hs[2 * width : 3 * width, n : n + CHUNK], preferred_element_type=f32)
        pieces.append(piece[0:token_count])
    after = jnp.concatenate(pieces, axis=1)
    after_out[...] = after.astype(bf16)
    after_copy = pltpu.make_async_copy(after_out, after_hbm, out_sems.at[orows])
    after_copy.start()
    flux_in = rms_norm(after, flux_gain_ref[...]).astype(bf16)
    rows[OWN] = lax.dot_general(
        wflux_ref[...], flux_in, (((1,), (1,)), ((), ())), preferred_element_type=f32
    ).astype(bf16)

    def rows_at(side):
        return rows.at[side]

    start_both(3, rows.at[OWN], rows_at)

    wait_both(1, land_ref, land_at)
    for side, base in ((FAST, 0), (OWN, orows), (SLOW, 2 * orows)):
        for i in range(orows):
            place = base + i
            if side == OWN:
                at = local_row(place)
            else:
                at = odd * i + even * (orows - 1 - i)
            cells = land[side, pl.ds(at, 1), :].astype(f32)
            sea[place, :, 0:tail] = cells[:, 0:tail]
            sea[place, :, tail:] = jnp.concatenate(
                [cells[:, tail:], jnp.zeros((1, wide - olon), f32)], axis=1)
    @pl.when(has_slow)
    def _():
        for place in (2 * orows - 1, 2 * orows - 2):
            halo_copy(SLOW, place).wait()

    def state_part(place, n):
        block = xs[pl.ds(pl.multiple_of((place - 1) * 3 * opad, 16), 9 * opad), n : n + CHUNK]
        return jnp.dot(w_state[:, 0 : 9 * opad], block, preferred_element_type=f32)

    def keep_state(place, carry):
        for n in range(0, wide, CHUNK):
            kept[pl.ds(pl.multiple_of((place - 1) * hid, 16), hid), n : n + CHUNK] = state_part(
                place, n)
        return carry

    def keep_first(i, carry):
        spread_state(2 * orows + i, 0)
        for j in range(2):
            keep_state(1 + 2 * i + j, 0)
        return carry

    lax.fori_loop(0, 2, keep_first, 0)
    wait_both(3, rows.at[OWN], rows_at)
    sources = [rows[side].astype(f32) for side in range(3)]
    for i in range(orows):
        at = local_row(orows + i)
        regridded = jnp.zeros_like(sources[0])
        for side, device in ((FAST, fast), (OWN, me), (SLOW, slow)):
            weight = jnp.float32(0.0)
            for b in range(flux_weight.shape[0]):
                weight = weight + jnp.where(
                    flux_first[at] + b == device, flux_weight[b, at], 0.0)
            regridded = regridded + weight * sources[side]
        mid[OWN, i] = regridded.astype(bf16)

    def mid_at(side):
        return mid.at[side]

    start_both(4, mid.at[OWN], mid_at)

    @pl.when(has_slow)
    def _():
        for place in range(2 * orows - 3, orows - 1, -1):
            halo_copy(SLOW, place).start()

    lax.fori_loop(orows + 1, 2 * orows + 1, keep_state, 0, unroll=2)
    wait_both(4, mid.at[OWN], mid_at)
    every = [mid[FAST, orows - 1 - i] for i in range(orows)]
    every += [mid[OWN, i] for i in range(orows)]
    every += [mid[SLOW, orows - 1 - i] for i in range(orows)]
    repeated = jnp.dot(
        jnp.concatenate(every, axis=0), repeat[...], preferred_element_type=f32).astype(bf16)
    for place in range(3 * orows):
        base = place * 3 * nflux
        whole = repeated[place * nflux : (place + 1) * nflux]
        fx[base + nflux : base + 2 * nflux, :] = whole
        fx[base : base + nflux, :] = pltpu.roll(whole, 1, 1)
        fx[base + 2 * nflux : base + 3 * nflux, :] = pltpu.roll(whole, wide - 1, 1)

    root = (2.0 / jnp.pi) ** 0.5

    def inside_of(place):
        row = me * orows + local_row(place)
        return (row >= 0) & (row < total_rows)

    def first(step, place, both=False):
        half = jnp.where(inside_of(place), 0.5, 0.0).astype(f32)
        at = pl.ds(pl.multiple_of((place - 1) * hid, 16), hid)
        for n in range(0, wide, CHUNK):
            if step == 0:
                block = fx[
                    pl.ds(pl.multiple_of((place - 1) * 3 * nflux, 16), 9 * nflux), n : n + CHUNK]
                share = jnp.dot(w_flux[...], block, preferred_element_type=f32)
                full = share + (state_part(place, n) if both else kept[at, n : n + CHUNK])
                kept[at, n : n + CHUNK] = share
            else:
                full = kept[at, n : n + CHUNK] + state_part(place, n)
            bent = jnp.tanh(full * (root + (root * 0.044715) * (full * full)))
            half_full = full * half
            hidden = half_full + half_full * bent
            hs[pl.ds(pl.multiple_of((place + 1) * 3 * hid + hid, 16), hid), n : n + CHUNK] = (
                hidden.astype(bf16))

    def second(step, place):
        for n in range(0, wide, CHUNK):
            block = hs[pl.ds(pl.multiple_of(place * 3 * hid, 16), 9 * hid), n : n + CHUNK]
            full = jnp.dot(w_second[...], block, preferred_element_type=f32)
            center = pl.ds(pl.multiple_of(place * 3 * opad + opad, 16), opad)
            if step == 0:
                before = xs[center, n : n + CHUNK].astype(f32)
            else:
                before = st[place - orows, :, n : n + CHUNK]
            state = before + sea[place, :, n : n + CHUNK] * full
            if step == OSTEPS - 1:
                for t in range(CHUNK // 128):
                    at = pl.ds(pl.multiple_of(local_row(place) * opad, 16), opad)
                    line[n // 128 + t, at, :] = state[
                        :, t * 128 : (t + 1) * 128]
            else:
                if orows <= place < 2 * orows:
                    st[place - orows, :, n : n + CHUNK] = state
                xs[center, n : n + CHUNK] = state.astype(bf16)

    last = 3 * orows - 3

    def first_one(k, carry):
        for i in range(2):
            spread_hidden(2 * k - 1 + i)
        for i in range(2):
            first(0, 1 + 2 * k + i)
        return carry

    def finished(place):
        at = pl.ds(pl.multiple_of(local_row(place) * opad, 16), opad)
        return pltpu.make_async_copy(
            line.at[:, at, :], line_hbm.at[:, at, :], out_sems.at[place - orows])

    lax.fori_loop(0, (last - 1) // 2, first_one, 0)
    for place in range(2, last - 1):
        if place < 4:
            spread_hidden(last - 4 + place)
        else:
            spread_state(place - 2, 0)
        second(0, place)
    for place in range(3, last - 2):
        if place < 5:
            spread_state(last - 6 + place, 0)
        else:
            spread_hidden(place - 2)
        first(1, place)

    @pl.when(has_slow)
    def _():
        for place in range(2 * orows - 3, orows - 1, -1):
            halo_copy(SLOW, place).wait()

    for place in (last + 1, last + 2):
        spread_state(place, 0)
    for place in (last - 4, last - 3):
        spread_hidden(place)
    for place in (last, last + 1):
        first(0, place, True)
    for place in (last, last + 1):
        spread_hidden(place)
    for place in range(orows, last - 3):
        second(1, place)
        finished(place).start()
    for place in (last - 1, last):
        second(0, place)
    for place in (last - 1, last):
        spread_state(place, 0)
    for place in (last - 2, last - 1):
        first(1, place)
    for place in (last - 2, last - 1):
        spread_hidden(place)
    for place in range(last - 3, last - 1):
        second(1, place)
        finished(place).start()
    for place in range(orows, last - 1):
        finished(place).wait()
    after_copy.wait()


def output_kernel(after_hbm, line_hbm, atmos_hbm, ocean_hbm, after, line, ocean, in_sems, out_sems):
    och, orows, olon = ocean.shape
    tiles = line.shape[0]
    opad = line.shape[1] // orows
    per_step = CHUNK // 128
    after_in = pltpu.make_async_copy(after_hbm, after, in_sems.at[tiles // per_step])
    after_out = pltpu.make_async_copy(after, atmos_hbm, out_sems.at[0])
    ocean_out = pltpu.make_async_copy(ocean, ocean_hbm, out_sems.at[1])
    ins = []
    for step in range(tiles // per_step):
        at = slice(step * per_step, (step + 1) * per_step)
        ins.append(pltpu.make_async_copy(line_hbm.at[at], line.at[at], in_sems.at[step]))
    for copy in ins:
        copy.start()
    after_in.start()
    for step in range(tiles // per_step):
        ins[step].wait()
        begin = step * CHUNK
        end = min(begin + CHUNK, olon)
        for c in range(och):
            cells = [
                line[step * per_step + t, pl.ds(c, orows, stride=opad), :] for t in range(per_step)]
            cells = jnp.concatenate(cells, axis=1)[:, 0 : end - begin]
            ocean[c, :, begin:end] = cells.astype(ocean.dtype)
    ocean_out.start()
    after_in.wait()
    after_out.start()
    ocean_out.wait()
    after_out.wait()


def local(
    atmos,
    ocean_state,
    land_mask,
    w_qkv,
    w_out,
    head_scale,
    gain_attn,
    gain_flux,
    w_flux,
    surf_embed,
    flux_start,
    flux_weight,
    surf_start,
    surf_weight,
    conv_first,
    conv_second,
):
    token_count, width = atmos.shape
    och, orows, olon = ocean_state.shape
    alon = olon // SPAN
    nflux = w_flux.shape[1]
    taps, hid, _ = conv_first.shape
    groups = width // GROUP
    per_group = GROUP // (width // head_scale.shape[0])
    padded = round_up(token_count, 16)
    key_pad = round_up(token_count, 128)
    opad = round_up(och, 16)
    wide = round_up(olon + 2, CHUNK)
    places = 3 * orows
    bf16 = jnp.bfloat16
    f32 = jnp.float32
    vmem = pl.BlockSpec(memory_space=pltpu.VMEM)
    smem = pl.BlockSpec(memory_space=pltpu.SMEM)
    anywhere = pl.BlockSpec(memory_space=pl.ANY)
    turned_shape = (round_up(taps * opad, 128), hid)
    after, line = pl.pallas_call(
        step_kernel,
        out_shape=[
            jax.ShapeDtypeStruct(atmos.shape, bf16),
            jax.ShapeDtypeStruct((wide // 128, orows * opad, 128), f32),
        ],
        in_specs=[smem] * 5 + [vmem] * 5 + [anywhere] * 6,
        out_specs=[anywhere] * 2,
        scratch_shapes=[
            pltpu.VMEM(ocean_state.shape, bf16),
            pltpu.VMEM(atmos.shape, bf16),
            pltpu.VMEM(atmos.shape, bf16),
            pltpu.VMEM((2, 3 * VARS * orows, alon), bf16),
            pltpu.VMEM((2, 3 * VARS * orows, 128), f32),
            pltpu.VMEM((orows - 2, opad, wide), bf16),
            pltpu.VMEM((taps, och + nflux, hid), bf16),
            pltpu.VMEM(conv_second.shape, bf16),
            pltpu.VMEM((3, VARS * orows, alon), bf16),
            pltpu.VMEM((2, padded, width), bf16),
            pltpu.VMEM((groups, padded, GROUP), bf16),
            pltpu.VMEM((2, groups, padded, GROUP), bf16),
            pltpu.VMEM((2, groups, padded, GROUP), bf16),
            pltpu.VMEM((2, per_group * key_pad, 128), bf16),
            pltpu.VMEM((2, per_group * key_pad, GROUP), bf16),
            pltpu.VMEM((2, padded, per_group * key_pad), bf16),
            pltpu.VMEM((head_scale.shape[0], padded, 128), f32),
            pltpu.VMEM((width // 128, padded, GROUP), f32),
            pltpu.VMEM((alon, wide), bf16),
            pltpu.VMEM((3, nflux, alon), bf16),
            pltpu.VMEM((3, orows, nflux, alon), bf16),
            pltpu.VMEM((3, orows, olon), jnp.int32),
            pltpu.VMEM((places, 1, wide), f32),
            pltpu.VMEM(atmos.shape, bf16),
            pltpu.VMEM((wide // 128, orows * opad, 128), f32),
            pltpu.VMEM((places * 3 * opad, wide), bf16),
            pltpu.VMEM((places * 3 * nflux, wide), bf16),
            pltpu.VMEM((places * 3 * hid, wide), bf16),
            pltpu.VMEM((orows, opad, wide), f32),
            pltpu.VMEM(((places - 2) * hid, wide), f32),
            pltpu.VMEM(turned_shape, f32),
            pltpu.VMEM((hid, turned_shape[0]), bf16),
            pltpu.VMEM((hid, taps * nflux), bf16),
            pltpu.VMEM((opad, taps * hid), bf16),
            pltpu.SemaphoreType.DMA((7,)),
            pltpu.SemaphoreType.DMA((orows + 1,)),
            pltpu.SemaphoreType.DMA((7, 3)),
            pltpu.SemaphoreType.DMA((7, 3)),
            pltpu.SemaphoreType.DMA((2, groups)),
            pltpu.SemaphoreType.DMA((2, groups)),
            pltpu.SemaphoreType.DMA((3, orows)),
            pltpu.SemaphoreType.DMA((3, orows)),
        ],
        compiler_params=pltpu.CompilerParams(
            collective_id=0, has_side_effects=True, vmem_limit_bytes=63 * 1024 * 1024
        ),
        name="coupled_step",
    )(surf_start, surf_weight, flux_start, flux_weight.T, head_scale, land_mask, surf_embed,
      gain_attn[None, :], gain_flux[None, :], w_flux.T, atmos, ocean_state, w_qkv, w_out,
      conv_first.transpose(0, 2, 1), conv_second)
    return pl.pallas_call(
        output_kernel,
        out_shape=[
            jax.ShapeDtypeStruct(atmos.shape, bf16),
            jax.ShapeDtypeStruct(ocean_state.shape, bf16),
        ],
        in_specs=[anywhere] * 2,
        out_specs=[anywhere] * 2,
        scratch_shapes=[
            pltpu.VMEM(atmos.shape, bf16),
            pltpu.VMEM(line.shape, f32),
            pltpu.VMEM(ocean_state.shape, bf16),
            pltpu.SemaphoreType.DMA((wide // CHUNK + 1,)),
            pltpu.SemaphoreType.DMA((2,)),
        ],
        name="outputs",
    )(after, line)


def solution(mesh):
    in_specs = (
        P(("ens", "lat"), None),
        P(None, ("ens", "lat"), None),
        P("lat", None),
        P(),
        P(),
        P(),
        P(),
        P(),
        P(),
        P(),
        P("lat"),
        P("lat", None),
        P("lat"),
        P("lat", None),
        P(),
        P(),
    )
    out_specs = (P(("ens", "lat"), None), P(None, ("ens", "lat"), None))
    return jax.shard_map(local, mesh=mesh, in_specs=in_specs, out_specs=out_specs, check_vma=False)
```

time: 77.4 us -> 71.9 us (0.929)
  local copies, waits for them, and re-layouts: 5.8 us -> 0 us
  Pallas kernels: 69.4 us -> 70.2 us
    unnamed x3 -> x0, local copies, waits for them, and re-layouts: 5.8 us -> none
    pallas_call x0 -> x1, Pallas kernels: none -> 2.89 us  [local(): pl.pallas_call(output_kernel, out_shape=[jax.ShapeDtypeStruct(atmos.shape...]
    pallas_call x1, Pallas kernels: 69.4 us -> 67.3 us  [local(): pl.pallas_call(step_kernel, out_shape=[jax.ShapeDtypeStruct(atmos.shape,...]
where the time goes in v2:
time: 71.9 us; the launch traced here: 71.6 us
  Pallas kernels  70.2 us (98%)
  between operations  1.47 us (2%)
    pallas_call x1, Pallas kernels, local(): pl.pallas_call(step_kernel, out_shape=[jax.ShapeDtypeStruct(atmos.shape,...  67.3 us
    pallas_call x1, Pallas kernels, local(): pl.pallas_call(output_kernel, out_shape=[jax.ShapeDtypeStruct(atmos.shape...  2.89 us

profile of v2, /device:TPU:20, one launch (start us, length us, event | category | flops | bytes accessed | tf_op | source)
XLA Modules:
  0.0 71.6 jit_solution(4772718832688648947)
XLA Ops:
  1.3 67.3 %coupled_step.1 = (bf16[360,1024]{1,0:T(8,128)(2,1)}, f32[12,320,128]{2,1,0:T(8,128)}) custom-call(s32[1]{0:T(128)S(6)} %copy.18.surf_first, f32[1,7]{1,0:T(1,128)} %surf_weight.1, s32[4]{0:T(128)} %flux_first.1, f32[2,4]{1,0:T(2,128)} %bitcast.9, f32[16]{0:T(128)} %scale_ref.1, s32[4,1440]{1,0:T(4,128)} %land_ref.1, f32[4,1024]{1,0:T(4,128)} %embed_ref.1, ...), custom_call_target="tpu_custom_call" | custom-call | tf_op jit(solution)/shard_map/coupled_step/pallas_call | solution.py:666
  68.6 2.9 %outputs.1 = (bf16[360,1024]{1,0:T(8,128)(2,1)}, bf16[76,4,1440]{2,1,0:T(4,128)(2,1)}) custom-call(bf16[360,1024]{1,0:T(8,128)(2,1)} %get-tuple-element.4.after_hbm, f32[12,320,128]{2,1,0:T(8,128)} %get-tuple-element.5.line_hbm), custom_call_target="tpu_custom_call" | custom-call | tf_op jit(solution)/shard_map/outputs/pallas_call | solution.py:725

commit v3 on v2

--- a/solution.py
+++ b/solution.py
@@ -26,7 +26,7 @@
                 gain_ref, flux_gain_ref, wflux_ref, atmos_hbm, ocean_hbm, qkv_hbm, wout_hbm,
                 first_hbm, second_hbm,
                 after_hbm, line_hbm,
-                ocean_in, atmos_in, atmos_near, fields, factors, edge, first_in, second_in, surf, near, queries, keys, vals, keys_wide,
+                ocean_in, atmos_in, atmos_near, factors, edge, first_in, second_in, surf, near, queries, keys, vals, keys_wide,
                 vals_wide, probs, largest_at, gathered, repeat, rows, mid, land, sea,
                 after_out, line, xs, fx, hs, st, kept, turned, w_state, w_flux, w_second,
                 load_sems, out_sems, send_sems, recv_sems, kv_send, kv_recv, halo_send, halo_recv):
@@ -55,6 +55,8 @@
     tail = wide - 128
     first_pad = olon - tail
     total_rows = count * orows
+    band = surf_weight.shape[1]
+    beyond_slow = slow - 1 + 2 * odd
     bf16 = jnp.bfloat16
     f32 = jnp.float32
 
@@ -119,6 +121,11 @@
     first_column = lax.broadcasted_iota(jnp.int32, (alon, wide), 0) * SPAN
     chosen = (longitude >= first_column) & (longitude < first_column + SPAN)
     repeat[...] = jnp.where(chosen, 1.0, 0.0).astype(bf16)
+    row_at = lax.broadcasted_iota(jnp.int32, factors.shape[1:], 0)
+    filled = jnp.where(row_at == band, surf_first[0].astype(f32), 0.0)
+    for b in range(band):
+        filled = jnp.where(row_at == b, surf_weight[0, b], filled)
+    factors[0] = filled
     loads[0].wait()
     top = jnp.concatenate(
         [ocean_in[v * LEVELS].astype(f32) for v in range(VARS)], axis=0).astype(bf16)
@@ -138,7 +145,7 @@
 
     @pl.when(has_slow)
     def _():
-        send(2, SLOW, atmos_hbm, atmos_near).start()
+        send(6, SLOW, factors.at[0], factors.at[1]).start()
 
     start_both(1, land_ref, land_at)
 
@@ -212,33 +219,37 @@
     embed = jnp.concatenate(
         [jnp.broadcast_to(embed_ref[v : v + 1, :], (orows, width)) for v in range(VARS)], axis=0)
     which = lax.broadcasted_iota(jnp.int32, (VARS * orows, 128), 0) % orows
-    for part, device in enumerate((fast, me, slow)):
-        weights = jnp.zeros((VARS * orows, 128), f32)
-        for i in range(orows):
-            column = device * orows + i
-            weight = jnp.float32(0.0)
-            for b in range(surf_weight.shape[1]):
-                weight = weight + jnp.where(surf_first[0] + b == column, surf_weight[0, b], 0.0)
-            weight = jnp.where((column >= 0) & (column < total_rows), weight, 0.0)
-            weights = jnp.where(which == i, weight, weights)
-        factors[0, part * VARS * orows : (part + 1) * VARS * orows, :] = weights
-
-    def start_of(tokens, whose):
-        scaled = factors[whose, :, 0:1] * jnp.concatenate([embed] * 3, axis=0)
+
+    def start_of(tokens, whose, parts, devices):
+        starts = factors[whose, band : band + 1, :]
+        scaled = []
+        for device in devices:
+            column = which + device * orows
+            weights = jnp.zeros((VARS * orows, 128), f32)
+            for b in range(band):
+                weights = weights + jnp.where(
+                    column.astype(f32) == starts + b, factors[whose, b : b + 1, :], 0.0)
+            weights = jnp.where((column >= 0) & (column < total_rows), weights, 0.0)
+            scaled.append(jnp.concatenate([weights] * (width // 128), axis=1) * embed)
+        scaled = jnp.concatenate(scaled, axis=0)
         high = scaled.astype(bf16)
         rest = scaled - high.astype(f32)
         middle = rest.astype(bf16)
         low = (rest - middle.astype(f32)).astype(bf16)
+        fields = jnp.concatenate([surf[part] for part in parts] * 3, axis=0)
         started = tokens[...].astype(f32) + lax.dot_general(
-            jnp.concatenate([fields[whose]] * 3, axis=0),
-            jnp.concatenate([high, middle, low], axis=0),
+            fields, jnp.concatenate([high, middle, low], axis=0),
             (((0,), (0,)), ((), ())), preferred_element_type=f32)
         return jnp.concatenate([started, jnp.zeros((padded - token_count, width), f32)], axis=0)
 
     loads[1].wait()
     wait_both(0, surf.at[OWN], surf_at)
-    fields[0] = jnp.concatenate([surf[FAST], surf[OWN], surf[SLOW]], axis=0)
-    started = start_of(atmos_in, 0)
+
+    @pl.when(has_slow)
+    def _():
+        send(2, SLOW, atmos_hbm, atmos_near).start()
+
+    started = start_of(atmos_in, 0, (FAST, OWN, SLOW), (fast, me, slow))
     held = kept.at[0:padded, 0:width]
     held[...] = started
     near[0] = rms_norm(started, gain_ref[...]).astype(bf16)
@@ -257,11 +268,9 @@
 
     @pl.when(has_slow)
     def _():
-        send(5, SLOW, fields.at[0], fields.at[1]).start()
-        send(6, SLOW, factors.at[0], factors.at[1]).start()
-
-    middle_row = round_up(padded // 2, 16)
-    blocks = (slice(0, middle_row), slice(middle_row, padded))
+        send(5, SLOW, surf.at[FAST], surf.at[3]).start()
+
+    blocks = (slice(0, padded),)
     ones_at = lax.broadcasted_iota(jnp.int32, (GROUP, 128), 0) % 128 // depth
     ones = jnp.where(ones_at == half_lane, 1.0, 0.0).astype(bf16)
 
@@ -374,11 +383,12 @@
     @pl.when(has_slow)
     def _():
         send(2, SLOW, atmos_hbm, atmos_near).wait()
-        send(5, SLOW, fields.at[0], fields.at[1]).wait()
+        send(5, SLOW, surf.at[FAST], surf.at[3]).wait()
         send(6, SLOW, factors.at[0], factors.at[1]).wait()
         for place in (2 * orows - 1, 2 * orows - 2):
             halo_copy(SLOW, place).start()
-        near[1] = rms_norm(start_of(atmos_near, 1), gain_ref[...]).astype(bf16)
+        near[1] = rms_norm(start_of(
+            atmos_near, 1, (3, SLOW, OWN), (beyond_slow, slow, me)), gain_ref[...]).astype(bf16)
 
     def fast_rows(i, carry):
         halo_copy(FAST, orows + i).wait()
@@ -421,6 +431,7 @@
 
     start_both(3, rows.at[OWN], rows_at)
 
+
     wait_both(1, land_ref, land_at)
     for side, base in ((FAST, 0), (OWN, orows), (SLOW, 2 * orows)):
         for i in range(orows):
@@ -473,13 +484,14 @@
 
     start_both(4, mid.at[OWN], mid_at)
 
+    lax.fori_loop(orows + 1, 2 * orows + 1, keep_state, 0, unroll=2)
+    wait_both(4, mid.at[OWN], mid_at)
+
     @pl.when(has_slow)
     def _():
         for place in range(2 * orows - 3, orows - 1, -1):
             halo_copy(SLOW, place).start()
 
-    lax.fori_loop(orows + 1, 2 * orows + 1, keep_state, 0, unroll=2)
-    wait_both(4, mid.at[OWN], mid_at)
     every = [mid[FAST, orows - 1 - i] for i in range(orows)]
     every += [mid[OWN, i] for i in range(orows)]
     every += [mid[SLOW, orows - 1 - i] for i in range(orows)]
@@ -564,6 +576,12 @@
             spread_hidden(place - 2)
         first(1, place)
 
+    for place in (last - 4, last - 3):
+        spread_hidden(place)
+    for place in range(orows, last - 3):
+        second(1, place)
+        finished(place).start()
+
     @pl.when(has_slow)
     def _():
         for place in range(2 * orows - 3, orows - 1, -1):
@@ -571,15 +589,10 @@
 
     for place in (last + 1, last + 2):
         spread_state(place, 0)
-    for place in (last - 4, last - 3):
-        spread_hidden(place)
     for place in (last, last + 1):
         first(0, place, True)
     for place in (last, last + 1):
         spread_hidden(place)
-    for place in range(orows, last - 3):
-        second(1, place)
-        finished(place).start()
     for place in (last - 1, last):
         second(0, place)
     for place in (last - 1, last):
@@ -675,12 +688,11 @@
             pltpu.VMEM(ocean_state.shape, bf16),
             pltpu.VMEM(atmos.shape, bf16),
             pltpu.VMEM(atmos.shape, bf16),
-            pltpu.VMEM((2, 3 * VARS * orows, alon), bf16),
-            pltpu.VMEM((2, 3 * VARS * orows, 128), f32),
+            pltpu.VMEM((2, round_up(surf_weight.shape[1] + 1, 8), 128), f32),
             pltpu.VMEM((orows - 2, opad, wide), bf16),
             pltpu.VMEM((taps, och + nflux, hid), bf16),
             pltpu.VMEM(conv_second.shape, bf16),
-            pltpu.VMEM((3, VARS * orows, alon), bf16),
+            pltpu.VMEM((4, VARS * orows, alon), bf16),
             pltpu.VMEM((2, padded, width), bf16),
             pltpu.VMEM((groups, padded, GROUP), bf16),
             pltpu.VMEM((2, groups, padded, GROUP), bf16),

time: 71.9 us -> 66.5 us (0.925)
  Pallas kernels: 70.2 us -> 64.2 us
    pallas_call x1, Pallas kernels: 67.3 us -> 61.3 us  [local(): pl.pallas_call(step_kernel, out_shape=[jax.ShapeDtypeStruct(atmos.shape,...]
where the time goes in v3:
time: 66.5 us; the launch traced here: 65.6 us
  Pallas kernels  64.2 us (97%)
  between operations  1.47 us (2%)
    pallas_call x1, Pallas kernels, local(): pl.pallas_call(step_kernel, out_shape=[jax.ShapeDtypeStruct(atmos.shape,...  61.3 us
    pallas_call x1, Pallas kernels, local(): pl.pallas_call(output_kernel, out_shape=[jax.ShapeDtypeStruct(atmos.shape...  2.89 us

profile of v3, /device:TPU:20, one launch (start us, length us, event | category | flops | bytes accessed | tf_op | source)
XLA Modules:
  0.0 65.6 jit_solution(7084453613799742373)
XLA Ops:
  1.3 61.3 %coupled_step.1 = (bf16[360,1024]{1,0:T(8,128)(2,1)}, f32[12,320,128]{2,1,0:T(8,128)}) custom-call(s32[1]{0:T(128)S(6)} %copy.18.surf_first, f32[1,7]{1,0:T(1,128)} %surf_weight.1, s32[4]{0:T(128)} %flux_first.1, f32[2,4]{1,0:T(2,128)} %bitcast.9, f32[16]{0:T(128)} %scale_ref.1, s32[4,1440]{1,0:T(4,128)} %land_ref.1, f32[4,1024]{1,0:T(4,128)} %embed_ref.1, ...), custom_call_target="tpu_custom_call" | custom-call | tf_op jit(solution)/shard_map/coupled_step/pallas_call | solution.py:679
  62.6 2.9 %outputs.1 = (bf16[360,1024]{1,0:T(8,128)(2,1)}, bf16[76,4,1440]{2,1,0:T(4,128)(2,1)}) custom-call(bf16[360,1024]{1,0:T(8,128)(2,1)} %get-tuple-element.4.after_hbm, f32[12,320,128]{2,1,0:T(8,128)} %get-tuple-element.5.line_hbm), custom_call_target="tpu_custom_call" | custom-call | tf_op jit(solution)/shard_map/outputs/pallas_call | solution.py:737

commit v4 on v3

--- a/solution.py
+++ b/solution.py
@@ -269,6 +269,8 @@
     @pl.when(has_slow)
     def _():
         send(5, SLOW, surf.at[FAST], surf.at[3]).start()
+        for place in (2 * orows - 1, 2 * orows - 2):
+            halo_copy(SLOW, place).start()
 
     blocks = (slice(0, padded),)
     ones_at = lax.broadcasted_iota(jnp.int32, (GROUP, 128), 0) % 128 // depth
@@ -385,14 +387,8 @@
         send(2, SLOW, atmos_hbm, atmos_near).wait()
         send(5, SLOW, surf.at[FAST], surf.at[3]).wait()
         send(6, SLOW, factors.at[0], factors.at[1]).wait()
-        for place in (2 * orows - 1, 2 * orows - 2):
-            halo_copy(SLOW, place).start()
         near[1] = rms_norm(start_of(
             atmos_near, 1, (3, SLOW, OWN), (beyond_slow, slow, me)), gain_ref[...]).astype(bf16)
-
-    def fast_rows(i, carry):
-        halo_copy(FAST, orows + i).wait()
-        return spread_state(orows - 1 - i, carry)
 
     def from_slow(g, slot):
         column = g * GROUP
@@ -406,8 +402,11 @@
     def _():
         by_two(from_slow)
 
-    lax.fori_loop(0, orows, fast_rows, 0)
+    for place in range(orows, 2 * orows):
+        halo_copy(FAST, place).wait()
     loads[4].wait()
+    for place in range(orows):
+        spread_state(place, 0)
 
     for t in range(width // 128):
         near[0, :, t * 128 : (t + 1) * 128] = (

time: 66.5 us -> 65.8 us (0.989)
  no operation moved by 1% of the time
where the time goes in v4:
time: 65.8 us; the launch traced here: 65.1 us
  Pallas kernels  63.6 us (97%)
  between operations  1.47 us (2%)
    pallas_call x1, Pallas kernels, local(): pl.pallas_call(step_kernel, out_shape=[jax.ShapeDtypeStruct(atmos.shape,...  60.7 us
    pallas_call x1, Pallas kernels, local(): pl.pallas_call(output_kernel, out_shape=[jax.ShapeDtypeStruct(atmos.shape...  2.89 us

profile of v4, /device:TPU:20, one launch (start us, length us, event | category | flops | bytes accessed | tf_op | source)
XLA Modules:
  0.0 65.1 jit_solution(7778469914085109380)
XLA Ops:
  1.3 60.7 %coupled_step.1 = (bf16[360,1024]{1,0:T(8,128)(2,1)}, f32[12,320,128]{2,1,0:T(8,128)}) custom-call(s32[1]{0:T(128)S(6)} %copy.18.surf_first, f32[1,7]{1,0:T(1,128)} %surf_weight.1, s32[4]{0:T(128)} %flux_first.1, f32[2,4]{1,0:T(2,128)} %bitcast.9, f32[16]{0:T(128)} %scale_ref.1, s32[4,1440]{1,0:T(4,128)} %land_ref.1, f32[4,1024]{1,0:T(4,128)} %embed_ref.1, ...), custom_call_target="tpu_custom_call" | custom-call | tf_op jit(solution)/shard_map/coupled_step/pallas_call | solution.py:678
  62.0 2.9 %outputs.1 = (bf16[360,1024]{1,0:T(8,128)(2,1)}, bf16[76,4,1440]{2,1,0:T(4,128)(2,1)}) custom-call(bf16[360,1024]{1,0:T(8,128)(2,1)} %get-tuple-element.4.after_hbm, f32[12,320,128]{2,1,0:T(8,128)} %get-tuple-element.5.line_hbm), custom_call_target="tpu_custom_call" | custom-call | tf_op jit(solution)/shard_map/outputs/pallas_call | solution.py:736
